TPU v7x, 32 devices: a whole 2x2x4 slice. The times are simulated.
32 devices in a mesh: group: 2 (over x), row: 8 (over z, y), expert: 2 (over core).
Axes of the slice: x: 2, y: 2, z: 4, core: 2. Of those that a mesh axis runs over, the one named last changes fastest.
Arguments:
- tokens: bfloat16 [2, 128, 128, 1024], P('group', ('row', 'expert')), parts along dimension 0, may hold values from -30 to 30
- ln_first: float32 [1024], replicated, may hold values from 0.5 to 1.5
- spec_first: bfloat16 [2, 8, 128, 128], replicated, may hold values from -0.375 to 0.375
- spec_second: bfloat16 [2, 8, 128, 128], replicated, may hold values from -0.375 to 0.375
- spec_bias: float32 [2, 1024], replicated, may hold values from -3 to 3
- ln_second: float32 [1024], replicated, may hold values from 0.5 to 1.5
- routing: int32 [2, 128, 128, 4], P('group', ('row', 'expert')), parts along dimension 0, may hold values from 0 to 3, as said below
- combine: float32 [2, 128, 128, 4], P('group', ('row', 'expert')), parts along dimension 0, may hold values from 0.1 to 0.6
- up_weight: bfloat16 [8, 1024, 1536], P('row'), may hold values from -0.1875 to 0.1875
- down_weight: bfloat16 [8, 1536, 1024], P('row'), may hold values from -0.109375 to 0.109375
Outputs:
- block_out: bfloat16 [2, 128, 128, 1024], P('group', ('row', 'expert')), parts along dimension 0
There are 2 independent parts, one for each index of `group`. A program takes and returns all parts, laid end to end along the dimension named above; an argument that names none is the same for every part. Nothing has to cross between parts.
Inputs may be any that keep to these rules, and one draw needn't show every extreme that they name: `routing`: each token names 4 different experts, and the 1024 tokens held by each index of row+expert name every expert exactly 1024 times.
All inputs are finite; a program needn't handle non-finite values.
Results may differ from a plain program's by a relative error of at most 0.006.
Values may be sent and summed in bfloat16 or wider, within the bound.
A program may use at most 128 MiB of HBM per device.

v0:
```python
import math

import jax
import jax.numpy as jnp
from jax import lax
from jax.sharding import PartitionSpec as P


def from_partner(value, axis, stride):
    mask = 2**stride
    pairs = [(source, source ^ mask) for source in range(lax.axis_size(axis))]
    return lax.ppermute(value, axis, pairs)


def twiddle(length):
    counter = jnp.arange(length, dtype=jnp.float32)
    angle = 2.0 * math.pi / length * jnp.mod(jnp.outer(counter, counter), float(length))
    return (jnp.cos(angle), jnp.sin(angle))


def layer_norm(values, gain):
    values = values.astype(jnp.float32)
    center = values - jnp.mean(values, axis=-1, keepdims=True)
    spread = jnp.mean(center * center, axis=-1, keepdims=True)
    return center * lax.rsqrt(spread + 1e-05) * gain


def product(left, right, form):
    return jnp.einsum(form, left, right, preferred_element_type=jnp.float32)


def complex_blocks(real_in, imag_in, weight):
    form = "ghkbi,bio->ghkbo"
    real_out = product(real_in, weight[0], form) - product(imag_in, weight[1], form)
    imag_out = product(real_in, weight[1], form) + product(imag_in, weight[0], form)
    return (real_out, imag_out)


def block_mlp(modes, first, second, bias):
    dims = modes.shape
    nblocks = first.shape[1]
    bwidth = first.shape[2]
    real_part = modes[:, 0].reshape(dims[0], dims[2], dims[3], nblocks, bwidth)
    imag_part = modes[:, 1].reshape(dims[0], dims[2], dims[3], nblocks, bwidth)
    hid_real, hid_imag = complex_blocks(real_part, imag_part, first)
    hid_real = jax.nn.relu(hid_real + bias[0].reshape(nblocks, bwidth)).astype(jnp.bfloat16)
    hid_imag = jax.nn.relu(hid_imag + bias[1].reshape(nblocks, bwidth)).astype(jnp.bfloat16)
    out_real, out_imag = complex_blocks(hid_real, hid_imag, second)
    return jnp.stack([out_real, out_imag], axis=1).reshape(dims).astype(jnp.bfloat16)


def run_expert(arrived, up_full, down_full):
    in_shape = arrived.shape
    width = arrived.shape[2]
    hidden = jax.nn.gelu(
        jnp.dot(arrived.reshape(-1, width), up_full, preferred_element_type=jnp.float32),
        approximate=True,
    ).astype(jnp.bfloat16)
    partial_out = jnp.dot(hidden, down_full, preferred_element_type=jnp.float32).reshape(
        in_shape[0], in_shape[1], width
    )
    return lax.all_to_all(
        partial_out.astype(jnp.bfloat16), "row", split_axis=0, concat_axis=0, tiled=True
    ).astype(partial_out.dtype)


def per_device(
    tokens,
    ln_first,
    spec_first,
    spec_second,
    spec_bias,
    ln_second,
    routing,
    combine,
    up_weight,
    down_weight,
):
    grid_len = tokens.shape[2]
    width = tokens.shape[3]
    cosine, sine = twiddle(grid_len)
    forward_cols = jnp.stack([cosine, -sine], axis=1).astype(jnp.bfloat16)
    forward_rows = jnp.stack(
        [jnp.stack([cosine, sine], axis=1), jnp.stack([-sine, cosine], axis=1)], axis=0
    ).astype(jnp.bfloat16)
    inverse_rows = jnp.stack(
        [jnp.stack([cosine, -sine], axis=1), jnp.stack([sine, cosine], axis=1)], axis=0
    ).astype(jnp.bfloat16)
    inverse_cols = jnp.stack([cosine, -sine], axis=0).astype(jnp.bfloat16)
    normed_first = layer_norm(tokens, ln_first).astype(jnp.bfloat16)
    col_spec = product(normed_first, forward_cols, "ghwd,wck->gchkd").astype(jnp.bfloat16)
    by_column = lax.all_to_all(col_spec, ("row", "expert"), split_axis=3, concat_axis=2, tiled=True)
    modes = (product(forward_rows, by_column, "amch,gchkd->gamkd") * (1.0 / grid_len)).astype(
        jnp.bfloat16
    )
    mixed_modes = block_mlp(modes, spec_first, spec_second, spec_bias)
    row_back = product(inverse_rows, mixed_modes, "amch,gchkd->gamkd").astype(jnp.bfloat16)
    by_row = lax.all_to_all(row_back, ("row", "expert"), split_axis=2, concat_axis=3, tiled=True)
    mixing = product(by_row, inverse_cols, "gchkd,ckw->ghwd") * (1.0 / grid_len)
    residual = (tokens.astype(jnp.float32) + mixing).astype(jnp.bfloat16)
    normed = layer_norm(residual, ln_second).astype(jnp.bfloat16).reshape(-1, width)
    n_tokens = normed.shape[0]
    top_count = routing.shape[-1]
    experts = lax.axis_size("row") // 2
    capacity = n_tokens * top_count // experts
    flat_route = routing.reshape(-1)
    one_hot = (flat_route[:, None] == jnp.arange(experts, dtype=jnp.int32)[None, :]).astype(
        jnp.int32
    )
    earlier = jnp.cumsum(one_hot, axis=0) - one_hot
    slot_index = flat_route * capacity + jnp.sum(earlier * one_hot, axis=1)
    token_of = jnp.arange(n_tokens * top_count, dtype=jnp.int32) // top_count
    source_row = jnp.zeros((experts * capacity,), jnp.int32).at[slot_index].set(token_of)
    send_rows = normed[source_row].reshape(experts, capacity, width)
    partner_up, partner_down = from_partner((up_weight, down_weight), "row", 0)
    up_full = jnp.concatenate([up_weight[0], partner_up[0]], axis=1)
    down_full = jnp.concatenate([down_weight[0], partner_down[0]], axis=0)
    outgoing = send_rows.reshape(experts * 2, capacity // 2, width)
    returned = run_expert(
        lax.all_to_all(outgoing, "row", split_axis=0, concat_axis=0, tiled=True), up_full, down_full
    )
    results = returned.reshape(experts, capacity, width)
    gathered = results.reshape(-1, width)[slot_index].reshape(n_tokens, top_count, width)
    moe_out = jnp.sum(gathered * combine.reshape(n_tokens, top_count, 1), axis=1)
    final = residual.reshape(-1, width).astype(jnp.float32) + moe_out
    return final.reshape(tokens.shape).astype(jnp.bfloat16)


def solution(mesh):
    placed = (
        P("group", ("row", "expert"), None, None),
        P(),
        P(),
        P(),
        P(),
        P(),
        P("group", ("row", "expert"), None, None),
        P("group", ("row", "expert"), None, None),
        P("row", None, None),
        P("row", None, None),
    )
    return jax.shard_map(
        per_device,
        mesh=mesh,
        in_specs=placed,
        out_specs=P("group", ("row", "expert"), None, None),
        check_vma=False,
    )
```

profile of v0, /device:TPU:0, one launch (start us, length us, event | category | flops | bytes accessed | tf_op | source)
XLA Modules:
  0.0 794.9 jit_solution(12745327477111533011)
XLA Ops:
  0.0 0.3 fusion.101
  0.3 2.1 convert_reduce_fusion.1
  2.4 2.3 fusion.22
  4.7 1.4 convert_bitcast_fusion
  6.1 4.3 copy.64
  10.4 7.8 all-to-all-start
  18.5 0.3 fusion.102
  18.8 76.7 %all-to-all-done = bf16[1,2,8,128,1024]{4,2,1,0,3:T(8,128)(2,1)} async-done(((bf16[1,2,8,128,1024]{4,2,1,0,3:T(8,128)(2,1)}), bf16[1,2,8,128,1024]{4,2,1,0,3:T(8,128)(2,1)}, u32[]{:S(2)}, u32[]{:S(2)}) %all-to-all-start) | async-done | bytes 4194336 | tf_op jit(solution)/shard_map/all_to_all | solution.py:92
  95.6 4.5 copy.137
  100.1 0.5 copy.66
  100.6 5.6 fusion.27
  106.1 0.4 fusion.124
  106.5 0.6 copy-done.3
  107.2 0.8 fusion.58
  108.0 0.8 fusion.60
  108.8 1.1 fusion.35
  110.0 1.1 fusion.49
  111.1 0.8 fusion.47
  111.9 1.1 fusion.33
  113.0 0.8 fusion.62
  113.9 0.7 fusion.65
  114.9 3.2 fusion.28
  118.1 11.2 %copy.80 = bf16[1,2,128,8,1024]{4,1,3,0,2:T(2,128)(2,1)} copy(bf16[1,2,128,8,1024]{2,4,1,3,0:T(8,128)(2,1)} %fusion.28) | data formatting | bytes 8388608 | tf_op jit(solution)/shard_map/convert_element_type | solution.py:97
  129.3 19.8 %all-to-all-start.1 = ((bf16[1,2,128,8,1024]{4,1,3,0,2:T(2,128)(2,1)}), bf16[1,2,128,8,1024]{4,1,3,0,2:T(2,128)(2,1)}, u32[]{:S(2)}, u32[]{:S(2)}) async-start(bf16[1,2,128,8,1024]{4,1,3,0,2:T(2,128)(2,1)} %copy.80), calls=%async_computation.1 | async-start | bytes 8388608 | tf_op jit(solution)/shard_map/all_to_all | solution.py:98
  150.0 1.2 reduce-window.6
  151.8 0.3 mul.277
  152.4 15.5 %scatter_custom_fusion = s32[4096]{0:T(1024)S(1)} fusion(s32[4096]{0:T(1024)S(1)} %bitcast.233, s32[4096]{0:T(1024)S(1)} %add_select_fusion.2, s32[]{:T(128)} %constant.50.clone.1), kind=kCustom, calls=%fused_computation.156 | custom fusion | bytes 16388 | tf_op jit(solution)/shard_map/scatter | solution.py:113
  167.9 0.3 negate_convert_fusion
  168.3 58.5 %all-to-all-done.1 = bf16[1,2,128,8,1024]{4,1,3,0,2:T(2,128)(2,1)} async-done(((bf16[1,2,128,8,1024]{4,1,3,0,2:T(2,128)(2,1)}), bf16[1,2,128,8,1024]{4,1,3,0,2:T(2,128)(2,1)}, u32[]{:S(2)}, u32[]{:S(2)}) %all-to-all-start.1) | async-done | bytes 4194336 | tf_op jit(solution)/shard_map/all_to_all | solution.py:98
  226.7 3.5 copy.81
  230.2 1.3 convert_reduce_fusion
  231.5 0.7 fusion.19
  232.2 0.6 copy-done.1
  232.8 0.7 fusion.21
  233.5 18.3 %gather_fusion = bf16[4096,1024]{1,0:T(8,128)(2,1)} fusion(bf16[1024,1024]{1,0:T(8,128)(2,1)S(1)} %bitcast.220, s32[4096]{0:T(1024)S(1)} %fusion.113), kind=kCustom, calls=%fused_computation | custom fusion | bytes 16793600 | tf_op jit(solution)/shard_map/gather | solution.py:114
  251.8 19.8 %all-to-all-start.2 = ((bf16[8,512,1024]{2,1,0:T(8,128)(2,1)}), bf16[8,512,1024]{2,1,0:T(8,128)(2,1)}, u32[]{:S(2)}, u32[]{:S(2)}) async-start(bf16[8,512,1024]{2,1,0:T(8,128)(2,1)} %bitcast.221), calls=%async_computation.2 | async-start | bytes 16777216 | tf_op jit(solution)/shard_map/all_to_all | solution.py:120
  271.6 2.0 collective-permute-start
  273.7 159.1 %collective-permute-done = bf16[1,1024,1536]{2,1,0:T(8,128)(2,1)} collective-permute-done((bf16[1,1024,1536]{2,1,0:T(8,128)(2,1)S(1)}, bf16[1,1024,1536]{2,1,0:T(8,128)(2,1)}, u32[]{:S(2)}, u32[]{:S(2)}) %collective-permute-start) | collective-permute-done | bytes 3145760 | tf_op jit(solution)/shard_map/ppermute | solution.py:12
  432.7 22.6 %all-to-all-done.2 = bf16[8,512,1024]{2,1,0:T(8,128)(2,1)} async-done(((bf16[8,512,1024]{2,1,0:T(8,128)(2,1)}), bf16[8,512,1024]{2,1,0:T(8,128)(2,1)}, u32[]{:S(2)}, u32[]{:S(2)}) %all-to-all-start.2) | async-done | bytes 8388640 | tf_op jit(solution)/shard_map/all_to_all | solution.py:120
  455.4 45.2 %fusion.7 = bf16[4096,3072]{1,0:T(8,128)(2,1)} fusion(bf16[4096,1024]{1,0:T(8,128)(2,1)} %bitcast.80, bf16[1024,1536]{1,0:T(8,128)(2,1)} %bitcast.82, bf16[1024,1536]{1,0:T(8,128)(2,1)S(1)} %bitcast.240), kind=kOutput, calls=%fused_computation.11 | convolution fusion | flops 25895632896 | bytes 39845888 | tf_op jit(solution)/shard_map/dot_general | solution.py:56
  500.6 32.6 %convolution_convert_fusion = bf16[4096,1024]{1,0:T(8,128)(2,1)} fusion(bf16[4096,3072]{1,0:T(8,128)(2,1)} %fusion.7, bf16[1536,1024]{1,0:T(8,128)(2,1)} %bitcast.84, bf16[1536,1024]{1,0:T(8,128)(2,1)} %bitcast.241), kind=kOutput, calls=%fused_computation.17 | convolution fusion | flops 25786580992 | bytes 39845888 | tf_op jit(solution)/shard_map/dot_general | solution.py:59
  533.2 5.1 all-to-all-start.3
  538.5 182.2 %all-to-all-done.3 = bf16[8,512,1024]{2,1,0:T(8,128)(2,1)} async-done(((bf16[8,512,1024]{2,1,0:T(8,128)(2,1)}), bf16[8,512,1024]{2,1,0:T(8,128)(2,1)}, u32[]{:S(2)}, u32[]{:S(2)}) %all-to-all-start.3) | async-done | bytes 8388640 | tf_op jit(solution)/shard_map/all_to_all | solution.py:62
  720.7 11.3 %bitcast_convert_fusion = f32[4096,1024]{1,0:T(8,128)} fusion(bf16[8,512,1024]{2,1,0:T(8,128)(2,1)} %all-to-all-done.3), kind=kLoop, calls=%fused_computation.13 | loop fusion | flops 4194304 | bytes 25165824 | tf_op jit(solution)/shard_map/reshape;reshape | solution.py:123
  732.0 28.1 %gather_fusion.1 = f32[4096,1024]{1,0:T(8,128)} fusion(f32[4096,1024]{1,0:T(8,128)} %bitcast_convert_fusion, s32[4096]{0:T(1024)S(1)} %broadcast_clamp_fusion), kind=kCustom, calls=%fused_computation.1 | custom fusion | bytes 33570816 | tf_op jit(solution)/shard_map/gather | solution.py:123
  760.1 19.0 %reshape.316 = f32[1024,4,1024]{2,1,0:T(4,128)} reshape(f32[4096,1024]{1,0:T(8,128)} %gather_fusion.1) | data formatting | bytes 33554432 | tf_op jit(solution)/shard_map/reshape | solution.py:123
  779.1 13.4 %multiply_reduce_fusion = f32[1024,1024]{1,0:T(8,128)S(1)} fusion(f32[1024,4,1024]{2,1,0:T(4,128)} %reshape.316, f32[1024,4]{1,0:T(8,128)S(1)} %copy.87), kind=kLoop, calls=%fused_computation.12 | loop fusion | flops 7340032 | bytes 20987904 | tf_op jit(solution)/shard_map/reduce_sum | solution.py:124
  792.5 2.1 fusion.26
  (51 shorter events, 2.7 us)
Async XLA Ops:
  0.0 4.7 copy-start
  0.0 4.7 copy-start.11
  10.4 8.4 %copy-start.9 = (f32[2,1024]{1,0:T(2,128)S(1)}, f32[2,1024]{1,0:T(2,128)}, u32[]{:S(2)}) copy-start(f32[2,1024]{1,0:T(2,128)} %param.14) | copy-start | bytes 24580
  10.4 85.1 %all-to-all-start = ((bf16[1,2,8,128,1024]{4,2,1,0,3:T(8,128)(2,1)}), bf16[1,2,8,128,1024]{4,2,1,0,3:T(8,128)(2,1)}, u32[]{:S(2)}, u32[]{:S(2)}) async-start(bf16[1,2,8,128,1024]{4,2,1,0,3:T(8,128)(2,1)} %copy.64), calls=%async_computation | async-start | bytes 8388608 | tf_op jit(solution)/shard_map/all_to_all | solution.py:92
  106.1 1.0 copy-start.3
  108.8 1.2 copy-start.4
  129.3 19.8 %copy-start.5 = (s32[1,8,128,4]{2,3,1,0:T(4,128)S(1)}, s32[1,8,128,4]{2,3,1,0:T(4,128)}, u32[]{:S(2)}) copy-start(s32[1,8,128,4]{2,3,1,0:T(4,128)} %param.16) | copy-start | bytes 49156
  129.3 97.4 %all-to-all-start.1 = ((bf16[1,2,128,8,1024]{4,1,3,0,2:T(2,128)(2,1)}), bf16[1,2,128,8,1024]{4,1,3,0,2:T(2,128)(2,1)}, u32[]{:S(2)}, u32[]{:S(2)}) async-start(bf16[1,2,128,8,1024]{4,1,3,0,2:T(2,128)(2,1)} %copy.80), calls=%async_computation.1 | async-start | bytes 8388608 | tf_op jit(solution)/shard_map/all_to_all | solution.py:98
  152.4 15.5 %copy-start.6 = (s32[4096,1]{0,1:T(1,128)}, s32[4096,1]{0,1:T(1,128)S(1)}, u32[]{:S(2)}) copy-start(s32[4096,1]{0,1:T(1,128)S(1)} %compare_select_fusion) | copy-start | bytes 49156
  230.2 2.6 copy-start.10
  231.5 1.3 copy-start.1
  251.8 19.8 %copy-start.12 = (bf16[1,1024,1536]{2,1,0:T(8,128)(2,1)S(1)}, bf16[1,1024,1536]{2,1,0:T(8,128)(2,1)}, u32[]{:S(2)}) copy-start(bf16[1,1024,1536]{2,1,0:T(8,128)(2,1)} %param.18) | copy-start | bytes 9437188
  251.8 203.6 %all-to-all-start.2 = ((bf16[8,512,1024]{2,1,0:T(8,128)(2,1)}), bf16[8,512,1024]{2,1,0:T(8,128)(2,1)}, u32[]{:S(2)}, u32[]{:S(2)}) async-start(bf16[8,512,1024]{2,1,0:T(8,128)(2,1)} %bitcast.221), calls=%async_computation.2 | async-start | bytes 16777216 | tf_op jit(solution)/shard_map/all_to_all | solution.py:120
  271.6 161.2 %collective-permute-start = (bf16[1,1024,1536]{2,1,0:T(8,128)(2,1)S(1)}, bf16[1,1024,1536]{2,1,0:T(8,128)(2,1)}, u32[]{:S(2)}, u32[]{:S(2)}) collective-permute-start(bf16[1,1024,1536]{2,1,0:T(8,128)(2,1)S(1)} %copy-done.12), channel_id=1, source_target_pairs={{0,2},{2,0},{4,6},{6,4},{8,10},{10,8},{12,14},{14,12},{1,3},{3,1},... | collective-permute-start | bytes 9437192 | tf_op jit(solution)/shard_map/ppermute | solution.py:12
  273.6 227.0 %collective-permute-start.1 = (bf16[1,1536,1024]{2,1,0:T(8,128)(2,1)}, bf16[1,1536,1024]{2,1,0:T(8,128)(2,1)}, u32[]{:S(2)}, u32[]{:S(2)}) collective-permute-start(bf16[1,1536,1024]{2,1,0:T(8,128)(2,1)} %param.19), channel_id=1, source_target_pairs={{0,2},{2,0},{4,6},{6,4},{8,10},{10,8},{12,14},{14,12},{1,3},{3,1},... | collective-permute-start | bytes 9437192 | tf_op jit(solution)/shard_map/ppermute | solution.py:12
  533.2 5.1 copy-start.8
  533.2 5.3 copy-start.7
  533.2 187.6 %all-to-all-start.3 = ((bf16[8,512,1024]{2,1,0:T(8,128)(2,1)}), bf16[8,512,1024]{2,1,0:T(8,128)(2,1)}, u32[]{:S(2)}, u32[]{:S(2)}) async-start(bf16[8,512,1024]{2,1,0:T(8,128)(2,1)} %bitcast.228), calls=%async_computation.3 | async-start | bytes 16777216 | tf_op jit(solution)/shard_map/all_to_all | solution.py:62
  779.1 13.4 %copy-start.2 = (bf16[1,8,128,1024]{3,2,1,0:T(8,128)(2,1)S(1)}, bf16[1,8,128,1024]{3,2,1,0:T(8,128)(2,1)}, u32[]{:S(2)}) copy-start(bf16[1,8,128,1024]{3,2,1,0:T(8,128)(2,1)} %copy-done.1) | copy-start | bytes 6291460
where the time goes:
time: 801 us; the launch traced here: 795 us
  waiting for transfers between devices  499 us (62%)
  local copies, waits for them, and re-layouts  109 us (14%)
  matrix products  96.5 us (12%)
  starting transfers between devices  54.6 us (7%)
  other arithmetic  35.4 us (4%)
    all_to_all x1, waiting for transfers between devices, run_expert(): lax.all_to_all(partial_out.astype(jnp.bfloat16), 'row', split_axis=0, con...  182 us
    ppermute x2, waiting for transfers between devices, from_partner(): return lax.ppermute(value, axis, pairs)  159 us
    all_to_all x1, waiting for transfers between devices, per_device(): lax.all_to_all(col_spec, ('row', 'expert'), split_axis=3, concat_axis=2,...  76.7 us
    all_to_all x1, waiting for transfers between devices, per_device(): lax.all_to_all(row_back, ('row', 'expert'), split_axis=2, concat_axis=3,...  58.5 us
    dot_general x1, matrix products, run_expert(): jnp.dot(arrived.reshape(-1, width), up_full, preferred_element_type=jnp.f...  45.2 us
    dot_general x1, matrix products, run_expert(): jnp.dot(hidden, down_full, preferred_element_type=jnp.float32)  32.6 us
    gather x1, local copies, waits for them, and re-layouts, per_device(): results.reshape(-1, width)[slot_index].reshape(n_tokens, top_count, width)  28.1 us
    all_to_all x1, waiting for transfers between devices, per_device(): lax.all_to_all(outgoing, 'row', split_axis=0, concat_axis=0, tiled=True)  22.6 us
  transfers between devices with their start and end apart: 6, of which 5 were waited for; matrix products, arithmetic and copies ran while one was open for 8% of the time, Pallas kernels for 0%

commit v1 on v0

--- a/solution.py
+++ b/solution.py
@@ -2,7 +2,11 @@
 
 import jax
 import jax.numpy as jnp
+import numpy as np
 from jax import lax
+from jax.experimental import pallas as pl
+from jax.experimental.pallas import tpu as pltpu
+from jax.sharding import Mesh
 from jax.sharding import PartitionSpec as P
 
 
@@ -126,23 +130,258 @@
     return final.reshape(tokens.shape).astype(jnp.bfloat16)
 
 
+RING = ("ex", "half", "expert")
+
+
+def mixer_kernel(slots, bwidth, scale, x_ref, d_ref, dt_ref, w1_ref, w2_ref, bias_ref, out_ref):
+    rows, lanes = x_ref.shape
+    grid_len = rows // (2 * slots)
+    ranks = grid_len // 8
+    x = x_ref[...].astype(jnp.float32).reshape(ranks, 2 * slots, 8, lanes)
+    real_parts, imag_parts = [], []
+    for slot in range(slots):
+        pair = jnp.concatenate(
+            [
+                x[:, slot].reshape(grid_len, lanes),
+                x[:, slots + slot].reshape(grid_len, lanes),
+            ],
+            axis=0,
+        ).astype(jnp.bfloat16)
+        modes = jnp.dot(d_ref[slot], pair, preferred_element_type=jnp.float32) * scale
+        modes = modes.astype(jnp.bfloat16)
+        real_parts.append(modes[: 2 * grid_len])
+        imag_parts.append(modes[2 * grid_len :])
+    real = jnp.concatenate(real_parts, axis=0)
+    imag = jnp.concatenate(imag_parts, axis=0)
+    mixed_real, mixed_imag = [], []
+    for block in range(lanes // bwidth):
+        cut = slice(block * bwidth, (block + 1) * bwidth)
+        both = jnp.concatenate([real[:, cut], imag[:, cut]], axis=1)
+        hid = jnp.dot(both, w1_ref[block], preferred_element_type=jnp.float32) + bias_ref[block]
+        hid = jnp.maximum(hid, 0.0).astype(jnp.bfloat16)
+        mixed = jnp.dot(hid, w2_ref[block], preferred_element_type=jnp.float32).astype(jnp.bfloat16)
+        mixed_real.append(mixed[:, :bwidth])
+        mixed_imag.append(mixed[:, bwidth:])
+    real = jnp.concatenate(mixed_real, axis=1)
+    imag = jnp.concatenate(mixed_imag, axis=1)
+    back_real, back_imag = [], []
+    for slot in range(slots):
+        cut = slice(slot * 2 * grid_len, (slot + 1) * 2 * grid_len)
+        column = jnp.concatenate([real[cut], imag[cut]], axis=0)
+        back = jnp.dot(dt_ref[slot], column, preferred_element_type=jnp.float32)
+        back_real.append(back[:grid_len].reshape(ranks, 8, lanes))
+        back_imag.append(back[grid_len:].reshape(ranks, 8, lanes))
+    out = jnp.stack(back_real + back_imag, axis=1).reshape(rows, lanes)
+    out_ref[...] = out.astype(jnp.bfloat16)
+
+
+def mixer(x, d, dt, w1, w2, bias, slots, scale):
+    rows, width = x.shape
+    nblocks, twice = w1.shape[:2]
+    bwidth = twice // 2
+    per_step = 2
+    lanes = per_step * bwidth
+    whole = lambda i: (0, 0, 0)
+    weights = pl.BlockSpec((per_step, twice, twice), lambda i: (i, 0, 0))
+    body = lambda *refs: mixer_kernel(slots, bwidth, scale, *refs)
+    return pl.pallas_call(
+        body,
+        grid=(nblocks // per_step,),
+        in_specs=[
+            pl.BlockSpec((rows, lanes), lambda i: (0, i)),
+            pl.BlockSpec(d.shape, whole),
+            pl.BlockSpec(dt.shape, whole),
+            weights,
+            weights,
+            pl.BlockSpec((per_step, 1, twice), lambda i: (i, 0, 0)),
+        ],
+        out_specs=pl.BlockSpec((rows, lanes), lambda i: (0, i)),
+        out_shape=jax.ShapeDtypeStruct((rows, width), jnp.bfloat16),
+        name="mixer",
+    )(x, d, dt, w1, w2, bias)
+
+
+def complex_square(weight):
+    top = jnp.concatenate([weight[0], weight[1]], axis=2)
+    low = jnp.concatenate([-weight[1], weight[0]], axis=2)
+    return jnp.concatenate([top, low], axis=1)
+
+
+def swap(value, mask):
+    count = lax.axis_size("ex")
+    return lax.ppermute(value, "ex", [(e, e ^ mask) for e in range(count)])
+
+
+def expert_ffn(rows, up, down):
+    total = None
+    for part in range(up.shape[0]):
+        hidden = jax.nn.gelu(
+            jnp.dot(rows, up[part], preferred_element_type=jnp.float32), approximate=True
+        ).astype(jnp.bfloat16)
+        out = jnp.dot(hidden, down[part], preferred_element_type=jnp.float32)
+        total = out if total is None else total + out
+    return total
+
+
+def per_device_dense(
+    tokens,
+    ln_first,
+    spec_first,
+    spec_second,
+    spec_bias,
+    ln_second,
+    routing,
+    combine,
+    up_weight,
+    down_weight,
+):
+    _, my_rows, grid_len, width = tokens.shape
+    n_tokens = my_rows * grid_len
+    ranks = grid_len // my_rows
+    slots = grid_len // 2 // ranks
+    experts = lax.axis_size("ex")
+    copies = lax.axis_size("group") * lax.axis_size("expert")
+    me = lax.axis_index(RING)
+    my_expert = lax.axis_index("ex")
+
+    share = lax.axis_index("group") * lax.axis_size("expert") + lax.axis_index("expert")
+    up_rows = up_weight.shape[1] // copies
+    down_rows = down_weight.shape[1] // copies
+    up_piece = lax.dynamic_slice_in_dim(up_weight[0], share * up_rows, up_rows, 0)
+    down_piece = lax.dynamic_slice_in_dim(down_weight[0], share * down_rows, down_rows, 0)
+    held = []
+    for mask in range(0, experts, 2):
+        piece_up = up_piece if mask == 0 else swap(up_piece, mask)
+        piece_down = down_piece if mask == 0 else swap(down_piece, mask)
+        names = ("half", "group", "expert")
+        full_up = lax.all_gather(piece_up, names, axis=0, tiled=True)
+        full_down = lax.all_gather(piece_down, names, axis=0, tiled=True)
+        held.append(
+            (
+                full_up.reshape((2,) + up_weight.shape[1:]),
+                full_down.reshape((2,) + down_weight.shape[1:]),
+            )
+        )
+
+    route = routing.reshape(n_tokens, -1)
+    gate = combine.reshape(n_tokens, -1)
+    by_expert = jnp.stack(
+        [jnp.sum(jnp.where(route == e, gate, 0.0), axis=1) for e in range(experts)], axis=0
+    )
+    by_expert_other = swap(by_expert, 1)
+
+    cosine, sine = twiddle(grid_len)
+    half = grid_len // 2
+    first_col = (jnp.arange(half) == 0)[:, None]
+    packed = jnp.stack(
+        [cosine[:half], jnp.where(first_col, cosine[half][None], -sine[:half])], axis=0
+    ).astype(jnp.bfloat16)
+    packed = packed.reshape(2, ranks, slots, grid_len).transpose(1, 0, 2, 3)
+    eye = jnp.eye(my_rows, dtype=jnp.bfloat16)
+    columns = (packed[:, :, :, None, None, :] * eye[None, None, None, :, :, None]).reshape(
+        n_tokens, n_tokens
+    )
+    normed_first = layer_norm(tokens, ln_first).astype(jnp.bfloat16).reshape(n_tokens, width)
+    col_spec = jnp.dot(columns, normed_first, preferred_element_type=jnp.float32)
+    col_spec = col_spec.astype(jnp.bfloat16)
+    by_column = lax.all_to_all(col_spec, RING, split_axis=0, concat_axis=0, tiled=True)
+
+    none = jnp.zeros_like(cosine)
+    usual = jnp.concatenate(
+        [
+            jnp.concatenate([cosine, sine], axis=1),
+            jnp.concatenate([cosine, -sine], axis=1),
+            jnp.concatenate([-sine, cosine], axis=1),
+            jnp.concatenate([-sine, -cosine], axis=1),
+        ],
+        axis=0,
+    )
+    real_pair = jnp.concatenate(
+        [
+            jnp.concatenate([cosine, none], axis=1),
+            jnp.concatenate([none, cosine], axis=1),
+            jnp.concatenate([-sine, none], axis=1),
+            jnp.concatenate([none, -sine], axis=1),
+        ],
+        axis=0,
+    )
+    is_first = ((jnp.arange(slots) == 0) & (me == 0))[:, None, None]
+    rows_matrix = jnp.where(is_first, real_pair[None], usual[None]).astype(jnp.bfloat16)
+    nblocks, bwidth = spec_first.shape[1:3]
+    bias = jnp.concatenate(
+        [spec_bias[0].reshape(nblocks, 1, bwidth), spec_bias[1].reshape(nblocks, 1, bwidth)], axis=2
+    )
+    row_back = mixer(
+        by_column,
+        rows_matrix,
+        rows_matrix.transpose(0, 2, 1),
+        complex_square(spec_first),
+        complex_square(spec_second),
+        bias,
+        slots,
+        1.0 / grid_len,
+    )
+    by_row = lax.all_to_all(row_back, RING, split_axis=0, concat_axis=0, tiled=True)
+    mixing = lax.dot_general(
+        columns, by_row, (((0,), (0,)), ((), ())), preferred_element_type=jnp.float32
+    ) * (1.0 / grid_len)
+    residual = (tokens.reshape(n_tokens, width).astype(jnp.float32) + mixing).astype(jnp.bfloat16)
+    normed = layer_norm(residual, ln_second).astype(jnp.bfloat16)
+
+    pieces = CHUNKS
+    step = n_tokens // pieces
+    arrived = [swap(normed[p * step : (p + 1) * step], 1) for p in range(pieces)]
+
+    def weighted(rows, gates, index):
+        expert = my_expert ^ (2 * index)
+        gate_row = lax.dynamic_index_in_dim(gates, expert, axis=0, keepdims=False)
+        return gate_row[:, None] * expert_ffn(rows, *held[index])
+
+    own = residual.astype(jnp.float32)
+    for index in range(len(held)):
+        own = own + weighted(normed, by_expert, index)
+    returned = []
+    for p in range(pieces):
+        gates = by_expert_other[:, p * step : (p + 1) * step]
+        total = weighted(arrived[p], gates, 0)
+        for index in range(1, len(held)):
+            total = total + weighted(arrived[p], gates, index)
+        returned.append(swap(total.astype(jnp.bfloat16), 1))
+    final = own + jnp.concatenate(returned, axis=0).astype(jnp.float32)
+    return final.reshape(tokens.shape).astype(jnp.bfloat16)
+
+
+CHUNKS = 2
+
+
 def solution(mesh):
-    placed = (
-        P("group", ("row", "expert"), None, None),
-        P(),
-        P(),
-        P(),
-        P(),
-        P(),
-        P("group", ("row", "expert"), None, None),
-        P("group", ("row", "expert"), None, None),
-        P("row", None, None),
-        P("row", None, None),
-    )
-    return jax.shard_map(
-        per_device,
-        mesh=mesh,
-        in_specs=placed,
-        out_specs=P("group", ("row", "expert"), None, None),
-        check_vma=False,
-    )
+    shape = mesh.shape
+    group, row, expert = shape["group"], shape["row"], shape["expert"]
+    split = Mesh(
+        np.asarray(mesh.devices).reshape(group, row // 2, 2, expert),
+        ("group", "ex", "half", "expert"),
+    )
+
+    def placed(row_names):
+        cells = P("group", row_names + ("expert",), None, None)
+        weights = P(row_names, None, None)
+        return (cells, P(), P(), P(), P(), P(), cells, cells, weights, weights), cells
+
+    def run(*args):
+        experts = row // 2
+        tokens, routing = args[0], args[6]
+        ranks = row * expert
+        dense = routing.shape[-1] == experts and experts % 4 == 0
+        dense = dense and tokens.shape[1] == 8 * ranks and (tokens.shape[2] // 2) % ranks == 0
+        dense = dense and tokens.shape[0] == group and args[8].shape[1] % (group * expert) == 0
+        if dense:
+            ins, outs = placed(("ex", "half"))
+            call = jax.shard_map(
+                per_device_dense, mesh=split, in_specs=ins, out_specs=outs, check_vma=False
+            )
+        else:
+            ins, outs = placed(("row",))
+            call = jax.shard_map(per_device, mesh=mesh, in_specs=ins, out_specs=outs, check_vma=False)
+        return call(*args)
+
+    return run

time: 801 us -> 398 us (0.50)
  waiting for transfers between devices: 499 us -> 189 us
  local copies, waits for them, and re-layouts: 109 us -> 11.3 us
  matrix products: 96.5 us -> 125 us
  starting transfers between devices: 54.6 us -> 29.6 us
  other arithmetic: 35.4 us -> 14.1 us
  between operations: 0.68 us -> 13.9 us
  Pallas kernels: 0 us -> 8.37 us
    all_to_all x4 -> x2, waiting for transfers between devices: 340 us -> 31.9 us  [the longest x1 31.9 us: per_device_dense(): lax.all_to_all(col_spec, RING, split_axis=0, concat_axis=0, tiled=True)]
    gather x2 -> x0, local copies, waits for them, and re-layouts: 46.4 us -> none  [the longest x1 28.1 us: per_device(): results.reshape(-1, width)[slot_index].reshape(n_tokens, top_count, width)]
    all_to_all x4 -> x2, starting transfers between devices: 52.5 us -> 17.5 us  [the longest x1 11.6 us: per_device_dense(): lax.all_to_all(row_back, RING, split_axis=0, concat_axis=0, tiled=True)]
    dot_general x14, matrix products: 96.5 us -> 125 us  [the longest x12 117 us: expert_ffn(): out = jnp.dot(hidden, down[part], preferred_element_type=jnp.float32)]
    reshape x1 -> x0, local copies, waits for them, and re-layouts: 19 us -> none  [per_device(): results.reshape(-1, width)[slot_index].reshape(n_tokens, top_count, width)]
    scatter x1 -> x0, local copies, waits for them, and re-layouts: 15.5 us -> none  [per_device(): jnp.zeros((experts * capacity,), jnp.int32).at[slot_index].set(token_of)]
    convert_element_type x2 -> x0, local copies, waits for them, and re-layouts: 15.5 us -> none  [the longest x1 11.2 us: per_device(): product(inverse_rows, mixed_modes, 'amch,gchkd->gamkd').astype(jnp.bfloat16)]
    reduce_sum x2 -> x1, other arithmetic: 13.5 us -> 0.05 us  [per_device_dense(): jnp.sum(jnp.where(route == e, gate, 0.0), axis=1)]
  transfers between devices with their start and end apart: 6 -> 13, of which waited for: 5 -> 6; matrix products, arithmetic and copies ran while one was open for 8% -> 29% of each run, Pallas kernels for 0% -> 2%
where the time goes in v1:
time: 398 us; the launch traced here: 392 us
  waiting for transfers between devices  189 us (47%)
  matrix products  125 us (31%)
  starting transfers between devices  29.6 us (7%)
  other arithmetic  14.1 us (4%)
  between operations  13.9 us (3%)
  local copies, waits for them, and re-layouts  11.3 us (3%)
  Pallas kernels  8.37 us (2%)
    ppermute x7, waiting for transfers between devices, swap(): return lax.ppermute(value, 'ex', [(e, e ^ mask) for e in range(count)])  157 us
    dot_general x12, matrix products, expert_ffn(): out = jnp.dot(hidden, down[part], preferred_element_type=jnp.float32)  117 us
    all_to_all x1, waiting for transfers between devices, per_device_dense(): lax.all_to_all(col_spec, RING, split_axis=0, concat_axis=0, tiled=True)  31.9 us
    all_to_all x1, starting transfers between devices, per_device_dense(): lax.all_to_all(row_back, RING, split_axis=0, concat_axis=0, tiled=True)  11.6 us
    ppermute x7, starting transfers between devices, swap(): return lax.ppermute(value, 'ex', [(e, e ^ mask) for e in range(count)])  11.5 us
    pallas_call x1, Pallas kernels, mixer(): pl.pallas_call(body, grid=(nblocks // per_step,), in_specs=[pl.BlockSpec(...  8.37 us
  transfers between devices with their start and end apart: 13, of which 6 were waited for; matrix products, arithmetic and copies ran while one was open for 29% of the time, Pallas kernels for 2%

profile of v1, /device:TPU:0, one launch (start us, length us, event | category | flops | bytes accessed | tf_op | source)
XLA Modules:
  0.0 391.7 jit_solution(8124477654648833391)
XLA Ops:
  6.5 1.9 copy-done
  8.4 1.0 constant_dynamic-slice_fusion.6
  9.5 2.1 constant_dynamic-slice_fusion.5
  11.7 4.1 %collective-permute-start = (bf16[256,1536]{1,0:T(8,128)(2,1)S(1)}, bf16[256,1536]{1,0:T(8,128)(2,1)S(1)}, u32[]{:S(2)}, u32[]{:S(2)}) collective-permute-start(bf16[256,1536]{1,0:T(8,128)(2,1)S(1)} %fusion.272), channel_id=1, source_target_pairs={{0,8},{4,12},{8,0},{12,4},{1,9},{5,13},{9,1},{13,5},{2,10},{6,14},... | collective-permute-start | bytes 2359304 | tf_op jit(solution)/shard_map/ppermute | solution.py:212
  15.9 34.4 %collective-permute-done = bf16[256,1536]{1,0:T(8,128)(2,1)S(1)} collective-permute-done((bf16[256,1536]{1,0:T(8,128)(2,1)S(1)}, bf16[256,1536]{1,0:T(8,128)(2,1)S(1)}, u32[]{:S(2)}, u32[]{:S(2)}) %collective-permute-start) | collective-permute-done | bytes 786464 | tf_op jit(solution)/shard_map/ppermute | solution.py:212
  50.3 0.9 copy-done.12
  51.2 0.9 fusion.197
  52.4 2.0 convert_reduce_fusion.1
  54.4 0.7 multiply_reduce_fusion
  55.2 0.7 broadcast_multiply_fusion
  55.9 0.7 multiply_convert_fusion
  56.6 3.7 fusion.156
  60.3 6.0 %all-to-all-start = ((bf16[16,64,1024]{2,1,0:T(8,128)(2,1)}), bf16[16,64,1024]{2,1,0:T(8,128)(2,1)}, u32[]{:S(2)}, u32[]{:S(2)}) async-start(bf16[16,64,1024]{2,1,0:T(8,128)(2,1)} %bitcast.125), calls=%async_computation | async-start | bytes 4194304 | tf_op jit(solution)/shard_map/all_to_all | solution.py:287
  66.6 1.5 fusion.254
  68.1 0.8 copy.13
  68.9 0.8 fusion.255
  69.7 0.8 copy.12
  71.4 1.7 maximum_maximum_fusion
  73.0 1.1 select_convert_fusion.refs_2_
  74.2 1.2 select_convert_fusion.1.refs_1_
  75.4 31.9 %all-to-all-done = bf16[16,64,1024]{2,1,0:T(8,128)(2,1)} async-done(((bf16[16,64,1024]{2,1,0:T(8,128)(2,1)}), bf16[16,64,1024]{2,1,0:T(8,128)(2,1)}, u32[]{:S(2)}, u32[]{:S(2)}) %all-to-all-start) | async-done | bytes 2097184 | tf_op jit(solution)/shard_map/all_to_all | solution.py:287
  107.4 8.4 %mixer.1 = bf16[1024,1024]{1,0:T(8,128)(2,1)} custom-call(bf16[1024,1024]{1,0:T(8,128)(2,1)} %bitcast.7.refs_0_, bf16[4,512,256]{2,1,0:T(8,128)(2,1)} %select_convert_fusion.1.refs_1_, bf16[4,256,512]{2,1,0:T(8,128)(2,1)} %select_convert_fusion.refs_2_, bf16[8,256,256]{2,1,0:T(8,128)(2,1)} %get-tuple-element.33.refs_3_, ...), custom_call_target="tpu_custom_call" | custom-call | tf_op jit(solution)/shard_map/mixer/pallas_call | solution.py:187
  115.7 11.6 %all-to-all-start.1 = ((bf16[16,64,1024]{2,1,0:T(8,128)(2,1)}), bf16[16,64,1024]{2,1,0:T(8,128)(2,1)}, u32[]{:S(2)}, u32[]{:S(2)}) async-start(bf16[16,64,1024]{2,1,0:T(8,128)(2,1)} %bitcast.121), calls=%async_computation.1 | async-start | bytes 4194304 | tf_op jit(solution)/shard_map/all_to_all | solution.py:324
  127.8 1.2 fusion.273
  129.0 2.8 collective-permute-start.1
  131.9 78.1 %collective-permute-done.1 = bf16[384,1024]{1,0:T(8,128)(2,1)S(1)} collective-permute-done((bf16[384,1024]{1,0:T(8,128)(2,1)S(1)}, bf16[384,1024]{1,0:T(8,128)(2,1)S(1)}, u32[]{:S(2)}, u32[]{:S(2)}) %collective-permute-start.1) | collective-permute-done | bytes 786464 | tf_op jit(solution)/shard_map/ppermute | solution.py:212
  210.0 0.9 copy-done.13
  211.0 5.0 %convert_reduce_fusion = (f32[1024]{0:T(1024)S(1)}, bf16[1024,1024]{1,0:T(8,128)(2,1)S(1)}) fusion(bf16[1024,1024]{1,0:T(8,128)(2,1)} %bitcast.17, bf16[128,8,8,128]{3,2,1,0:T(8,128)(2,1)} %bitcast.124, bf16[1,8,128,1024]{3,2,1,0:T(8,128)(2,1)S(1)} %copy-done.2), kind=kOutput, calls=%fused_computation.38 | convolution fusion | flops 2153774080 | bytes 8392704 | tf_op jit(solution)/shard_map/dot_general | solution.py:325
  215.9 0.7 fusion.34
  216.7 0.7 fusion.36
  217.4 1.4 fusion.256
  218.9 2.1 collective-permute-start.2
  221.0 23.0 %collective-permute-done.2 = f32[4,1024]{1,0:T(4,128)S(1)} collective-permute-done((f32[4,1024]{1,0:T(4,128)S(1)}, f32[4,1024]{1,0:T(4,128)S(1)}, u32[]{:S(2)}, u32[]{:S(2)}) %collective-permute-start.2) | collective-permute-done | bytes 16416 | tf_op jit(solution)/shard_map/ppermute | solution.py:212
  244.3 8.1 %fusion.117 = f32[512,1024]{1,0:T(8,128)} fusion(bf16[1,3072,1024]{2,1,0:T(8,128)(2,1)} %all-gather.13.cloned.1.call-done, bf16[512,1024]{1,0:T(8,128)(2,1)} %collective-permute-done.3, bf16[1,2048,1536]{2,1,0:T(8,128)(2,1)} %all-gather.11.cloned.1.call-done), kind=kOutput, calls=%fused_computation.136 | convolution fusion | flops 3228303360 | bytes 9437184 | tf_op jit(solution)/shard_map/dot_general | solution.py:221
  252.4 8.1 %fusion.122 = f32[512,1024]{1,0:T(8,128)} fusion(bf16[1,3072,1024]{2,1,0:T(8,128)(2,1)} %all-gather.13.cloned.1.call-done, bf16[512,1024]{1,0:T(8,128)(2,1)} %collective-permute-done.3, bf16[1,2048,1536]{2,1,0:T(8,128)(2,1)} %all-gather.11.cloned.1.call-done), kind=kOutput, calls=%fused_computation.141 | convolution fusion | flops 3228303360 | bytes 9437184 | tf_op jit(solution)/shard_map/dot_general | solution.py:221
  260.5 7.5 %collective-permute-done.5 = bf16[512,1024]{1,0:T(8,128)(2,1)} collective-permute-done((bf16[512,1024]{1,0:T(8,128)(2,1)S(1)}, bf16[512,1024]{1,0:T(8,128)(2,1)}, u32[]{:S(2)}, u32[]{:S(2)}) %collective-permute-start.5) | collective-permute-done | bytes 1048608 | tf_op jit(solution)/shard_map/ppermute | solution.py:212
  268.0 8.2 %fusion.116 = f32[512,1024]{1,0:T(8,128)} fusion(bf16[1,3072,1024]{2,1,0:T(8,128)(2,1)} %all-gather.13.cloned.1.call-done, bf16[512,1024]{1,0:T(8,128)(2,1)} %collective-permute-done.5, bf16[1,2048,1536]{2,1,0:T(8,128)(2,1)} %all-gather.11.cloned.1.call-done), kind=kOutput, calls=%fused_computation.135 | convolution fusion | flops 3228303360 | bytes 9437184 | tf_op jit(solution)/shard_map/dot_general | solution.py:221
  276.2 7.9 %fusion.121 = f32[512,1024]{1,0:T(8,128)} fusion(bf16[1,3072,1024]{2,1,0:T(8,128)(2,1)} %all-gather.13.cloned.1.call-done, bf16[512,1024]{1,0:T(8,128)(2,1)} %collective-permute-done.5, bf16[1,2048,1536]{2,1,0:T(8,128)(2,1)} %all-gather.11.cloned.1.call-done), kind=kOutput, calls=%fused_computation.140 | convolution fusion | flops 3228303360 | bytes 9437184 | tf_op jit(solution)/shard_map/dot_general | solution.py:221
  284.1 11.6 %fusion.109 = f32[1024,1024]{1,0:T(8,128)} fusion(bf16[1,3072,1024]{2,1,0:T(8,128)(2,1)} %all-gather.13.cloned.1.call-done, bf16[1024,1024]{1,0:T(8,128)(2,1)S(1)} %fusion.36, bf16[1,2048,1536]{2,1,0:T(8,128)(2,1)} %all-gather.11.cloned.1.call-done), kind=kOutput, calls=%fused_computation.130 | convolution fusion | flops 6456606720 | bytes 12582912 | tf_op jit(solution)/shard_map/dot_general | solution.py:221
  295.7 11.8 %fusion.111 = f32[1024,1024]{1,0:T(8,128)} fusion(bf16[1,3072,1024]{2,1,0:T(8,128)(2,1)} %all-gather.13.cloned.1.call-done, bf16[1024,1024]{1,0:T(8,128)(2,1)S(1)} %fusion.36, bf16[1,2048,1536]{2,1,0:T(8,128)(2,1)} %all-gather.11.cloned.1.call-done), kind=kOutput, calls=%fused_computation.131 | convolution fusion | flops 6456606720 | bytes 12582912 | tf_op jit(solution)/shard_map/dot_general | solution.py:221
  307.5 8.0 %fusion.125 = f32[512,1024]{1,0:T(8,128)} fusion(bf16[3072,1024]{1,0:T(8,128)(2,1)} %all-gather.9.cloned.1.call-done, bf16[512,1024]{1,0:T(8,128)(2,1)} %collective-permute-done.3, bf16[2048,1536]{1,0:T(8,128)(2,1)} %all-gather.7.cloned.1.call-done), kind=kOutput, calls=%fused_computation.144 | convolution fusion | flops 3228303360 | bytes 9437184 | tf_op jit(solution)/shard_map/dot_general | solution.py:221
  315.5 8.5 %add_convert_fusion.1 = bf16[512,1024]{1,0:T(8,128)(2,1)S(1)} fusion(f32[512,1024]{1,0:T(8,128)} %fusion.125, f32[512,1024]{1,0:T(8,128)} %fusion.117, f32[512,1024]{1,0:T(8,128)} %fusion.122, f32[512]{0:T(512)S(1)} %bitcast.136, f32[512]{0:T(512)S(1)} %bitcast.137, bf16[3072,1024]{1,0:T(8,128)(2,1)} %all-gather.9.cloned.1.call-done, ...), kind=kOutput, calls=%fused_computation.168 | convolution fusion | flops 3231449088 | bytes 14684160 | tf_op jit(solution)/shard_map/dot_general | solution.py:221
  324.7 8.0 %fusion.123 = f32[512,1024]{1,0:T(8,128)} fusion(bf16[3072,1024]{1,0:T(8,128)(2,1)} %all-gather.9.cloned.1.call-done, bf16[512,1024]{1,0:T(8,128)(2,1)} %collective-permute-done.5, bf16[2048,1536]{1,0:T(8,128)(2,1)} %all-gather.7.cloned.1.call-done), kind=kOutput, calls=%fused_computation.142 | convolution fusion | flops 3228303360 | bytes 9437184 | tf_op jit(solution)/shard_map/dot_general | solution.py:221
  332.7 9.9 %add_convert_fusion = bf16[512,1024]{1,0:T(8,128)(2,1)} fusion(f32[512,1024]{1,0:T(8,128)} %fusion.123, f32[512,1024]{1,0:T(8,128)} %fusion.116, f32[512,1024]{1,0:T(8,128)} %fusion.121, f32[512]{0:T(512)S(1)} %bitcast.135, f32[512]{0:T(512)S(1)} %bitcast.134, bf16[3072,1024]{1,0:T(8,128)(2,1)} %all-gather.9.cloned.1.call-done, ...), kind=kOutput, calls=%fused_computation.167 | convolution fusion | flops 3231449088 | bytes 14684160 | tf_op jit(solution)/shard_map/dot_general | solution.py:221
  342.6 1.5 collective-permute-start.6
  344.1 11.7 %fusion.105 = f32[1024,1024]{1,0:T(8,128)} fusion(bf16[3072,1024]{1,0:T(8,128)(2,1)} %all-gather.9.cloned.1.call-done, bf16[1024,1024]{1,0:T(8,128)(2,1)S(1)} %fusion.36, bf16[2048,1536]{1,0:T(8,128)(2,1)} %all-gather.7.cloned.1.call-done), kind=kOutput, calls=%fused_computation.128 | convolution fusion | flops 6456606720 | bytes 12582912 | tf_op jit(solution)/shard_map/dot_general | solution.py:221
  355.7 14.0 %collective-permute-done.6 = bf16[512,1024]{1,0:T(8,128)(2,1)} collective-permute-done((bf16[512,1024]{1,0:T(8,128)(2,1)}, bf16[512,1024]{1,0:T(8,128)(2,1)}, u32[]{:S(2)}, u32[]{:S(2)}) %collective-permute-start.6) | collective-permute-done | bytes 1048608 | tf_op jit(solution)/shard_map/ppermute | solution.py:212
  369.7 15.0 %fusion.39 = bf16[1024,1024]{1,0:T(8,128)(2,1)} fusion(bf16[1024,1024]{1,0:T(8,128)(2,1)} %copy-done.3, f32[1024,1024]{1,0:T(8,128)} %fusion.105, f32[1024,1024]{1,0:T(8,128)} %fusion.111, f32[1024,1024]{1,0:T(8,128)} %fusion.109, bf16[512,1024]{1,0:T(8,128)(2,1)} %collective-permute-done.6, bf16[512,1024]{1,0:T(8,128)(2,1)} %collective-permute-done.4, ...), kind=kOutput, calls=%fused_computation.54 | convolution fusion | flops 6470238208 | bytes 27271168 | tf_op jit(solution)/shard_map/dot_general | solution.py:221
  (77 shorter events, 3.3 us)
Async XLA Ops:
  6.5 1.9 copy-start
  6.5 237.8 %all-gather.11.cloned.1.call-start = ((), (), s32[]{:S(2)}) async-start(), calls=%async_computation.4 | async-start | bytes 7077888 | tf_op jit(solution)/shard_map/all_gather | solution.py:257
  9.4 234.9 %all-gather.13.cloned.1.call-start = ((), (), s32[]{:S(2)}) async-start(), calls=%async_computation.5 | async-start | bytes 7077888 | tf_op jit(solution)/shard_map/all_gather | solution.py:258
  11.6 295.9 %all-gather.7.cloned.1.call-start = ((), (), s32[]{:S(2)}) async-start(), calls=%async_computation.2 | async-start | bytes 7077888 | tf_op jit(solution)/shard_map/all_gather | solution.py:257
  11.7 42.7 %copy-start.2 = (bf16[1,8,128,1024]{3,2,1,0:T(8,128)(2,1)S(1)}, bf16[1,8,128,1024]{3,2,1,0:T(8,128)(2,1)}, u32[]{:S(2)}) copy-start(bf16[1,8,128,1024]{3,2,1,0:T(8,128)(2,1)} %param.10) | copy-start | bytes 6291460
  11.7 38.5 %collective-permute-start = (bf16[256,1536]{1,0:T(8,128)(2,1)S(1)}, bf16[256,1536]{1,0:T(8,128)(2,1)S(1)}, u32[]{:S(2)}, u32[]{:S(2)}) collective-permute-start(bf16[256,1536]{1,0:T(8,128)(2,1)S(1)} %fusion.272), channel_id=1, source_target_pairs={{0,8},{4,12},{8,0},{12,4},{1,9},{5,13},{9,1},{13,5},{2,10},{6,14},... | collective-permute-start | bytes 2359304 | tf_op jit(solution)/shard_map/ppermute | solution.py:212
  50.3 0.9 copy-start.12
  52.4 3.5 copy-start.17
  55.9 4.4 %copy-start.5 = (bf16[16,2,4,8,8,128]{5,4,3,2,1,0:T(8,128)(2,1)}, bf16[16,2,4,8,8,128]{5,4,3,2,1,0:T(8,128)(2,1)S(1)}, u32[]{:S(2)}) copy-start(bf16[16,2,4,8,8,128]{5,4,3,2,1,0:T(8,128)(2,1)S(1)} %broadcast_multiply_fusion) | copy-start | bytes 6291460
  60.3 10.2 %copy-start.16 = (f32[2,1024]{1,0:T(2,128)S(1)}, f32[2,1024]{1,0:T(2,128)}, u32[]{:S(2)}) copy-start(f32[2,1024]{1,0:T(2,128)} %param.14) | copy-start | bytes 24580
  60.3 10.9 %copy-start.7 = (bf16[2,8,128,128]{3,2,1,0:T(8,128)(2,1)S(1)}, bf16[2,8,128,128]{3,2,1,0:T(8,128)(2,1)}, u32[]{:S(2)}) copy-start(bf16[2,8,128,128]{3,2,1,0:T(8,128)(2,1)} %param.12) | copy-start | bytes 1572868
  60.3 10.9 %copy-start.6 = (bf16[2,8,128,128]{3,2,1,0:T(8,128)(2,1)S(1)}, bf16[2,8,128,128]{3,2,1,0:T(8,128)(2,1)}, u32[]{:S(2)}) copy-start(bf16[2,8,128,128]{3,2,1,0:T(8,128)(2,1)} %param.13) | copy-start | bytes 1572868
  60.3 47.1 %all-to-all-start = ((bf16[16,64,1024]{2,1,0:T(8,128)(2,1)}), bf16[16,64,1024]{2,1,0:T(8,128)(2,1)}, u32[]{:S(2)}, u32[]{:S(2)}) async-start(bf16[16,64,1024]{2,1,0:T(8,128)(2,1)} %bitcast.125), calls=%async_computation | async-start | bytes 4194304 | tf_op jit(solution)/shard_map/all_to_all | solution.py:287
  71.2 1.8 copy-start.10
  71.2 1.8 copy-start.11
  71.3 2.9 copy-start.8
  71.3 2.9 copy-start.9
  115.7 95.2 %all-to-all-start.1 = ((bf16[16,64,1024]{2,1,0:T(8,128)(2,1)}), bf16[16,64,1024]{2,1,0:T(8,128)(2,1)}, u32[]{:S(2)}, u32[]{:S(2)}) async-start(bf16[16,64,1024]{2,1,0:T(8,128)(2,1)} %bitcast.121), calls=%async_computation.1 | async-start | bytes 4194304 | tf_op jit(solution)/shard_map/all_to_all | solution.py:324
  127.3 180.2 %all-gather.9.cloned.1.call-start = ((), (), s32[]{:S(2)}) async-start(), calls=%async_computation.3 | async-start | bytes 7077888 | tf_op jit(solution)/shard_map/all_gather | solution.py:258
  129.0 81.0 %collective-permute-start.1 = (bf16[384,1024]{1,0:T(8,128)(2,1)S(1)}, bf16[384,1024]{1,0:T(8,128)(2,1)S(1)}, u32[]{:S(2)}, u32[]{:S(2)}) collective-permute-start(bf16[384,1024]{1,0:T(8,128)(2,1)S(1)} %fusion.273), channel_id=1, source_target_pairs={{0,8},{4,12},{8,0},{12,4},{1,9},{5,13},{9,1},{13,5},{2,10},{6,14},... | collective-permute-start | bytes 2359304 | tf_op jit(solution)/shard_map/ppermute | solution.py:212
  210.0 0.9 copy-start.13
  210.9 5.7 %copy-start.18 = (f32[1024]{0:T(1024)S(1)}, f32[1024]{0:T(1024)}, u32[]{:S(2)}) copy-start(f32[1024]{0:T(1024)} %param.15) | copy-start | bytes 12292
  215.9 1.4 copy-start.3
  217.4 126.7 %copy-start.4 = (bf16[1024,1024]{1,0:T(8,128)(2,1)}, bf16[1024,1024]{1,0:T(8,128)(2,1)S(1)}, u32[]{:S(2)}) copy-start(bf16[1024,1024]{1,0:T(8,128)(2,1)S(1)} %fusion.36) | copy-start | bytes 6291460
  217.4 1.4 copy-start.14
  217.4 1.4 copy-start.15
  218.8 25.5 %collective-permute-start.3 = (bf16[512,1024]{1,0:T(8,128)(2,1)}, bf16[512,1024]{1,0:T(8,128)(2,1)}, u32[]{:S(2)}, u32[]{:S(2)}) collective-permute-start(bf16[512,1024]{1,0:T(8,128)(2,1)} %get-tuple-element.9), channel_id=1, source_target_pairs={{0,4},{4,0},{8,12},{12,8},{1,5},{5,1},{9,13},{13,9},{2,6},{6,2},{1... | collective-permute-start | bytes 3145736 | tf_op jit(solution)/shard_map/ppermute | solution.py:212
  218.9 25.1 %collective-permute-start.2 = (f32[4,1024]{1,0:T(4,128)S(1)}, f32[4,1024]{1,0:T(4,128)S(1)}, u32[]{:S(2)}, u32[]{:S(2)}) collective-permute-start(f32[4,1024]{1,0:T(4,128)S(1)} %pad_maximum_fusion), channel_id=1, source_target_pairs={{0,4},{4,0},{8,12},{12,8},{1,5},{5,1},{9,13},{13,9},{2,6},{6,2},{1... | collective-permute-start | bytes 49160 | tf_op jit(solution)/shard_map/ppermute | solution.py:212
  244.0 24.0 %collective-permute-start.5 = (bf16[512,1024]{1,0:T(8,128)(2,1)S(1)}, bf16[512,1024]{1,0:T(8,128)(2,1)}, u32[]{:S(2)}, u32[]{:S(2)}) collective-permute-start(bf16[512,1024]{1,0:T(8,128)(2,1)S(1)} %get-tuple-element.10), channel_id=1, source_target_pairs={{0,4},{4,0},{8,12},{12,8},{1,5},{5,1},{9,13},{13,9},{2,6},{6,2},{1... | collective-permute-start | bytes 3145736 | tf_op jit(solution)/shard_map/ppermute | solution.py:212
  324.1 31.7 %collective-permute-start.4 = (bf16[512,1024]{1,0:T(8,128)(2,1)S(1)}, bf16[512,1024]{1,0:T(8,128)(2,1)}, u32[]{:S(2)}, u32[]{:S(2)}) collective-permute-start(bf16[512,1024]{1,0:T(8,128)(2,1)S(1)} %add_convert_fusion.1), channel_id=1, source_target_pairs={{0,4},{4,0},{8,12},{12,8},{1,5},{5,1},{9,13},{13,9},{2,6},{6,2},{1... | collective-permute-start | bytes 3145736 | tf_op jit(solution)/shard_map/ppermute | solution.py:212
  342.6 27.1 %collective-permute-start.6 = (bf16[512,1024]{1,0:T(8,128)(2,1)}, bf16[512,1024]{1,0:T(8,128)(2,1)}, u32[]{:S(2)}, u32[]{:S(2)}) collective-permute-start(bf16[512,1024]{1,0:T(8,128)(2,1)} %add_convert_fusion), channel_id=1, source_target_pairs={{0,4},{4,0},{8,12},{12,8},{1,5},{5,1},{9,13},{13,9},{2,6},{6,2},{1... | collective-permute-start | bytes 3145736 | tf_op jit(solution)/shard_map/ppermute | solution.py:212
  369.7 15.0 %copy-start.1 = (bf16[1,1024,1536]{2,1,0:T(8,128)(2,1)S(1)}, bf16[1,1024,1536]{2,1,0:T(8,128)(2,1)}, u32[]{:S(2)}) copy-start(bf16[1,1024,1536]{2,1,0:T(8,128)(2,1)} %param.18) | copy-start | bytes 9437188
Sparse Core Ops, SparseCore 0:
  9.6 48.1 all-gather.10
  59.6 66.5 all-gather.12
  128.1 57.4 all-gather.6
  211.1 44.3 all-gather.8

commit v2 on v1

--- a/solution.py
+++ b/solution.py
@@ -130,7 +130,7 @@
     return final.reshape(tokens.shape).astype(jnp.bfloat16)
 
 
-RING = ("ex", "half", "expert")
+RING = ("pair", "parity", "half", "expert")
 
 
 def mixer_kernel(slots, bwidth, scale, x_ref, d_ref, dt_ref, w1_ref, w2_ref, bias_ref, out_ref):
@@ -207,20 +207,73 @@
     return jnp.concatenate([top, low], axis=1)
 
 
-def swap(value, mask):
-    count = lax.axis_size("ex")
-    return lax.ppermute(value, "ex", [(e, e ^ mask) for e in range(count)])
-
-
-def expert_ffn(rows, up, down):
-    total = None
-    for part in range(up.shape[0]):
+def swap(value):
+    return lax.ppermute(value, "parity", [(0, 1), (1, 0)])
+
+
+def ffn_kernel(steps, x_ref, gate_ref, up_ref, down_ref, out_ref, part_ref, total_ref):
+    expert, step = pl.program_id(0), pl.program_id(1)
+    rows = x_ref.shape[0]
+    block = min(rows, 256)
+    for start in range(0, rows, block):
+        cut = pl.ds(start, block)
         hidden = jax.nn.gelu(
-            jnp.dot(rows, up[part], preferred_element_type=jnp.float32), approximate=True
+            jnp.dot(x_ref[cut, :], up_ref[0], preferred_element_type=jnp.float32), approximate=True
         ).astype(jnp.bfloat16)
-        out = jnp.dot(hidden, down[part], preferred_element_type=jnp.float32)
-        total = out if total is None else total + out
-    return total
+        out = jnp.dot(hidden, down_ref[0], preferred_element_type=jnp.float32)
+
+        @pl.when(step == 0)
+        def _():
+            part_ref[cut, :] = out
+
+        @pl.when(step > 0)
+        def _():
+            part_ref[cut, :] = part_ref[cut, :] + out
+
+    @pl.when(step == steps - 1)
+    def _():
+        lane = lax.broadcasted_iota(jnp.int32, gate_ref.shape, 1)
+        gate = jnp.sum(jnp.where(lane == expert, gate_ref[...], 0.0), axis=1, keepdims=True)
+        add = gate * part_ref[...]
+
+        @pl.when(expert == 0)
+        def _():
+            total_ref[...] = add
+
+        @pl.when(expert > 0)
+        def _():
+            total_ref[...] = total_ref[...] + add
+
+        @pl.when(expert == pl.num_programs(0) - 1)
+        def _():
+            out_ref[...] = total_ref[...].astype(out_ref.dtype)
+
+
+def expert_ffn(rows, gates, up, down, dtype):
+    count, width = rows.shape
+    experts = gates.shape[1]
+    halves, _, hidden = up.shape
+    cuts = 2
+    chunk = hidden // cuts
+    per = halves // experts
+    steps = per * cuts
+    return pl.pallas_call(
+        lambda *refs: ffn_kernel(steps, *refs),
+        grid=(experts, steps),
+        in_specs=[
+            pl.BlockSpec((count, width), lambda e, j: (0, 0)),
+            pl.BlockSpec((count, experts), lambda e, j: (0, 0)),
+            pl.BlockSpec((1, width, chunk), lambda e, j: (e * per + j // cuts, 0, j % cuts)),
+            pl.BlockSpec((1, chunk, width), lambda e, j: (e * per + j // cuts, j % cuts, 0)),
+        ],
+        out_specs=pl.BlockSpec((count, width), lambda e, j: (0, 0)),
+        out_shape=jax.ShapeDtypeStruct((count, width), dtype),
+        scratch_shapes=[
+            pltpu.VMEM((count, width), jnp.float32),
+            pltpu.VMEM((count, width), jnp.float32),
+        ],
+        name="ffn",
+    )(rows, gates, up, down)
 
 
 def per_device_dense(
@@ -239,36 +292,32 @@
     n_tokens = my_rows * grid_len
     ranks = grid_len // my_rows
     slots = grid_len // 2 // ranks
-    experts = lax.axis_size("ex")
+    pairs = lax.axis_size("pair")
     copies = lax.axis_size("group") * lax.axis_size("expert")
     me = lax.axis_index(RING)
-    my_expert = lax.axis_index("ex")
+    parity = lax.axis_index("parity")
 
     share = lax.axis_index("group") * lax.axis_size("expert") + lax.axis_index("expert")
     up_rows = up_weight.shape[1] // copies
     down_rows = down_weight.shape[1] // copies
     up_piece = lax.dynamic_slice_in_dim(up_weight[0], share * up_rows, up_rows, 0)
     down_piece = lax.dynamic_slice_in_dim(down_weight[0], share * down_rows, down_rows, 0)
-    held = []
-    for mask in range(0, experts, 2):
-        piece_up = up_piece if mask == 0 else swap(up_piece, mask)
-        piece_down = down_piece if mask == 0 else swap(down_piece, mask)
-        names = ("half", "group", "expert")
-        full_up = lax.all_gather(piece_up, names, axis=0, tiled=True)
-        full_down = lax.all_gather(piece_down, names, axis=0, tiled=True)
-        held.append(
-            (
-                full_up.reshape((2,) + up_weight.shape[1:]),
-                full_down.reshape((2,) + down_weight.shape[1:]),
-            )
-        )
+    names = ("pair", "half", "group", "expert")
+    up_all = lax.all_gather(up_piece, names, axis=0, tiled=True)
+    down_all = lax.all_gather(down_piece, names, axis=0, tiled=True)
+    up_all = up_all.reshape((2 * pairs,) + up_weight.shape[1:])
+    down_all = down_all.reshape((2 * pairs,) + down_weight.shape[1:])
 
     route = routing.reshape(n_tokens, -1)
     gate = combine.reshape(n_tokens, -1)
-    by_expert = jnp.stack(
-        [jnp.sum(jnp.where(route == e, gate, 0.0), axis=1) for e in range(experts)], axis=0
-    )
-    by_expert_other = swap(by_expert, 1)
+
+    def gates_for(side):
+        return jnp.stack(
+            [jnp.sum(jnp.where(route == 2 * e + side, gate, 0.0), axis=1) for e in range(pairs)]
+        )
+
+    own_gates = gates_for(parity).T
+    other_gates = swap(gates_for(1 - parity))
 
     cosine, sine = twiddle(grid_len)
     half = grid_len // 2
@@ -284,6 +333,8 @@
     normed_first = layer_norm(tokens, ln_first).astype(jnp.bfloat16).reshape(n_tokens, width)
     col_spec = jnp.dot(columns, normed_first, preferred_element_type=jnp.float32)
     col_spec = col_spec.astype(jnp.bfloat16)
+    col_spec, other_gates = lax.optimization_barrier((col_spec, other_gates))
+    other_gates = other_gates.T
     by_column = lax.all_to_all(col_spec, RING, split_axis=0, concat_axis=0, tiled=True)
 
     none = jnp.zeros_like(cosine)
@@ -328,40 +379,27 @@
     residual = (tokens.reshape(n_tokens, width).astype(jnp.float32) + mixing).astype(jnp.bfloat16)
     normed = layer_norm(residual, ln_second).astype(jnp.bfloat16)
 
-    pieces = CHUNKS
-    step = n_tokens // pieces
-    arrived = [swap(normed[p * step : (p + 1) * step], 1) for p in range(pieces)]
-
-    def weighted(rows, gates, index):
-        expert = my_expert ^ (2 * index)
-        gate_row = lax.dynamic_index_in_dim(gates, expert, axis=0, keepdims=False)
-        return gate_row[:, None] * expert_ffn(rows, *held[index])
-
-    own = residual.astype(jnp.float32)
-    for index in range(len(held)):
-        own = own + weighted(normed, by_expert, index)
-    returned = []
-    for p in range(pieces):
-        gates = by_expert_other[:, p * step : (p + 1) * step]
-        total = weighted(arrived[p], gates, 0)
-        for index in range(1, len(held)):
-            total = total + weighted(arrived[p], gates, index)
-        returned.append(swap(total.astype(jnp.bfloat16), 1))
-    final = own + jnp.concatenate(returned, axis=0).astype(jnp.float32)
+    step = n_tokens // 2
+    near, far = normed[:step], normed[step:]
+    first_in, second_in = swap(near), swap(far)
+    own_first = expert_ffn(near, own_gates[:step], up_all, down_all, jnp.float32)
+    first_in, own_first = lax.optimization_barrier((first_in, own_first))
+    first_out = expert_ffn(first_in, other_gates[:step], up_all, down_all, jnp.bfloat16)
+    first_back = swap(first_out)
+    second_in, first_out = lax.optimization_barrier((second_in, first_out))
+    second_out = expert_ffn(second_in, other_gates[step:], up_all, down_all, jnp.bfloat16)
+    second_back = swap(second_out)
+    far, second_out = lax.optimization_barrier((far, second_out))
+    own_second = expert_ffn(far, own_gates[step:], up_all, down_all, jnp.float32)
+    own = jnp.concatenate([own_first, own_second], axis=0)
+    back = jnp.concatenate([first_back, second_back], axis=0)
+    final = residual.astype(jnp.float32) + own + back.astype(jnp.float32)
     return final.reshape(tokens.shape).astype(jnp.bfloat16)
-
-
-CHUNKS = 2
 
 
 def solution(mesh):
     shape = mesh.shape
     group, row, expert = shape["group"], shape["row"], shape["expert"]
-    split = Mesh(
-        np.asarray(mesh.devices).reshape(group, row // 2, 2, expert),
-        ("group", "ex", "half", "expert"),
-    )
-
     def placed(row_names):
         cells = P("group", row_names + ("expert",), None, None)
         weights = P(row_names, None, None)
@@ -375,7 +413,11 @@
         dense = dense and tokens.shape[1] == 8 * ranks and (tokens.shape[2] // 2) % ranks == 0
         dense = dense and tokens.shape[0] == group and args[8].shape[1] % (group * expert) == 0
         if dense:
-            ins, outs = placed(("ex", "half"))
+            split = Mesh(
+                np.asarray(mesh.devices).reshape(group, row // 4, 2, 2, expert),
+                ("group", "pair", "parity", "half", "expert"),
+            )
+            ins, outs = placed(("pair", "parity", "half"))
             call = jax.shard_map(
                 per_device_dense, mesh=split, in_specs=ins, out_specs=outs, check_vma=False
             )

time: 398 us -> 425 us (1.068); the launches traced: 392 us -> 424 us
  matrix products: 125 us -> 6.42 us
  Pallas kernels: 8.37 us -> 108 us
  blocking collectives: 0 us -> 99.2 us
  waiting for transfers between devices: 189 us -> 153 us
  starting transfers between devices: 29.6 us -> 13.2 us
    ppermute x7 -> x5, waiting for transfers between devices: 157 us -> 30.1 us  [swap(): return lax.ppermute(value, 'parity', [(0, 1), (1, 0)])]
    dot_general x12 -> x0, matrix products: 117 us -> none  [expert_ffn(): out = jnp.dot(hidden, down[part], preferred_element_type=jnp.float32)]
    all_to_all x0 -> x1, blocking collectives: none -> 99.2 us  [per_device_dense(): lax.all_to_all(row_back, RING, split_axis=0, concat_axis=0, tiled=True)]
    pallas_call x0 -> x4, Pallas kernels: none -> 98.9 us  [expert_ffn(): pl.pallas_call(lambda *refs: ffn_kernel(steps, *refs), grid=(experts, ste...]
    all_gather x4 -> x2, waiting for transfers between devices: 0.01 us -> 68.8 us  [the longest x1 68.8 us: per_device_dense(): down_all = lax.all_gather(down_piece, names, axis=0, tiled=True)]
    all_to_all x1, waiting for transfers between devices: 31.9 us -> 54.4 us  [per_device_dense(): lax.all_to_all(col_spec, RING, split_axis=0, concat_axis=0, tiled=True)]
    all_to_all x1 -> x0, starting transfers between devices: 11.6 us -> none  [per_device_dense(): lax.all_to_all(row_back, RING, split_axis=0, concat_axis=0, tiled=True)]
    convert_element_type x0 -> x1, other arithmetic: none -> 4.93 us  [per_device_dense(): return final.reshape(tokens.shape).astype(jnp.bfloat16)]
  transfers between devices with their start and end apart: 13 -> 8, of which waited for: 6 -> 4; matrix products, arithmetic and copies ran while one was open for 29% -> 6% of each run, Pallas kernels for 2% -> 20%
where the time goes in v2:
time: 425 us; the launch traced here: 424 us
  waiting for transfers between devices  153 us (36%)
  Pallas kernels  108 us (25%)
  blocking collectives  99.2 us (23%)
  other arithmetic  17.2 us (4%)
  local copies, waits for them, and re-layouts  13.7 us (3%)
  between operations  13.7 us (3%)
  starting transfers between devices  13.2 us (3%)
  matrix products  6.42 us (2%)
    all_to_all x1, blocking collectives, per_device_dense(): lax.all_to_all(row_back, RING, split_axis=0, concat_axis=0, tiled=True)  99.2 us
    pallas_call x4, Pallas kernels, expert_ffn(): pl.pallas_call(lambda *refs: ffn_kernel(steps, *refs), grid=(experts, ste...  98.9 us
    all_gather x1, waiting for transfers between devices, per_device_dense(): down_all = lax.all_gather(down_piece, names, axis=0, tiled=True)  68.8 us
    all_to_all x1, waiting for transfers between devices, per_device_dense(): lax.all_to_all(col_spec, RING, split_axis=0, concat_axis=0, tiled=True)  54.4 us
    ppermute x5, waiting for transfers between devices, swap(): return lax.ppermute(value, 'parity', [(0, 1), (1, 0)])  30.1 us
    pallas_call x1, Pallas kernels, mixer(): pl.pallas_call(body, grid=(nblocks // per_step,), in_specs=[pl.BlockSpec(...  8.59 us
  transfers between devices with their start and end apart: 8, of which 4 were waited for; matrix products, arithmetic and copies ran while one was open for 6% of the time, Pallas kernels for 20%

profile of v2, /device:TPU:0, one launch (start us, length us, event | category | flops | bytes accessed | tf_op | source)
XLA Modules:
  0.0 424.3 jit_solution(4332876857752991233)
XLA Ops:
  6.5 1.9 copy-done
  8.4 0.9 constant_dynamic-slice_fusion.1
  9.5 2.2 constant_dynamic-slice_fusion
  11.8 0.2 copy.22
  12.0 3.1 collective-permute-start
  15.2 0.9 fusion.22
  16.1 0.3 fusion.21
  16.4 0.3 convert_reduce_fusion.1
  16.7 0.7 multiply_reduce_fusion
  17.4 0.1 fusion.25
  17.5 0.7 broadcast_multiply_fusion
  18.2 0.7 multiply_convert_fusion
  18.9 0.7 copy-done.5
  19.6 3.7 fusion.11
  23.3 8.7 %collective-permute-done = f32[2,1024]{0,1:T(8,128)S(1)} collective-permute-done((f32[2,1024]{0,1:T(8,128)S(1)}, f32[2,1024]{0,1:T(8,128)S(1)}, u32[]{:S(2)}, u32[]{:S(2)}) %collective-permute-start) | collective-permute-done | bytes 8224 | tf_op jit(solution)/shard_map/ppermute | solution.py:211
  32.0 0.8 copy-done.15
  32.8 5.4 %all-to-all-start = ((bf16[16,64,1024]{2,1,0:T(8,128)(2,1)}), bf16[16,64,1024]{2,1,0:T(8,128)(2,1)}, u32[]{:S(2)}, u32[]{:S(2)}) async-start(bf16[16,64,1024]{2,1,0:T(8,128)(2,1)} %bitcast.71), calls=%async_computation | async-start | bytes 4194304 | tf_op jit(solution)/shard_map/all_to_all | solution.py:338
  38.2 0.3 fusion.27
  38.5 1.5 fusion.31
  40.0 0.9 copy.24
  40.9 0.7 fusion.32
  41.6 0.8 copy.23
  42.5 0.6 pad_maximum_fusion.1.refs_5_
  43.3 1.6 maximum_maximum_fusion
  44.9 1.1 select_convert_fusion.refs_2_
  46.1 1.1 select_convert_fusion.1.refs_1_
  47.2 54.4 %all-to-all-done = bf16[16,64,1024]{2,1,0:T(8,128)(2,1)} async-done(((bf16[16,64,1024]{2,1,0:T(8,128)(2,1)}), bf16[16,64,1024]{2,1,0:T(8,128)(2,1)}, u32[]{:S(2)}, u32[]{:S(2)}) %all-to-all-start) | async-done | bytes 2097184 | tf_op jit(solution)/shard_map/all_to_all | solution.py:338
  101.6 8.6 %mixer.1 = bf16[1024,1024]{1,0:T(8,128)(2,1)} custom-call(bf16[1024,1024]{1,0:T(8,128)(2,1)} %bitcast.9.refs_0_, bf16[4,512,256]{2,1,0:T(8,128)(2,1)} %select_convert_fusion.1.refs_1_, bf16[4,256,512]{2,1,0:T(8,128)(2,1)} %select_convert_fusion.refs_2_, bf16[8,256,256]{2,1,0:T(8,128)(2,1)} %get-tuple-element.41.refs_3_, ...), custom_call_target="tpu_custom_call" | custom-call | tf_op jit(solution)/shard_map/mixer/pallas_call | solution.py:187
  110.2 99.2 %all_to_all.23 = bf16[16,64,1024]{2,1,0:T(8,128)(2,1)S(1)} all-to-all(bf16[16,64,1024]{2,1,0:T(8,128)(2,1)} %bitcast.67), channel_id=1, replica_groups=mesh['group'=2,'pair'=2,'parity'=2,'half'=2,'expert'=2] {'pair','parity'..., dimensions={0} | all-to-all | bytes 4194304 | tf_op jit(solution)/shard_map/all_to_all | solution.py:375
  209.5 2.8 convert_reduce_fusion
  212.3 0.7 fusion.2
  213.0 0.7 fusion.4
  213.7 1.1 fusion.33
  214.8 2.0 collective-permute-start.1
  216.8 0.1 collective-permute-start.2
  216.9 0.2 copy.25
  217.1 0.8 fusion.34
  217.9 1.9 fusion.35
  219.8 68.8 %all-gather.7.cloned.1.call-done = bf16[1,6144,1024]{2,1,0:T(8,128)(2,1)} async-done(((bf16[1,384,1024]{2,1,0:T(8,128)(2,1)}), bf16[1,6144,1024]{2,1,0:T(8,128)(2,1)}) %all-gather.7.cloned.1.call-update) | async-done | bytes 12582928 | tf_op jit(solution)/shard_map/all_gather | solution.py:307
  288.6 24.9 %ffn.4 = f32[512,1024]{1,0:T(8,128)} custom-call(bf16[512,1024]{1,0:T(8,128)(2,1)} %get-tuple-element.21.refs_0_, f32[512,2]{1,0:T(8,128)} %get-tuple-element.24.refs_1_, bf16[4,1024,1536]{2,1,0:T(8,128)(2,1)} %bitcast.59, bf16[4,1536,1024]{2,1,0:T(8,128)(2,1)} %bitcast.63), custom_call_target="tpu_custom_call" | custom-call | tf_op jit(solution)/shard_map/ffn/pallas_call | solution.py:260
  313.6 24.5 %ffn.5 = bf16[512,1024]{1,0:T(8,128)(2,1)} custom-call(bf16[512,1024]{1,0:T(8,128)(2,1)} %collective-permute-done.1.refs_0_, f32[512,2]{1,0:T(8,128)} %get-tuple-element.26.refs_1_, bf16[4,1024,1536]{2,1,0:T(8,128)(2,1)} %bitcast.60, bf16[4,1536,1024]{2,1,0:T(8,128)(2,1)} %bitcast.64), custom_call_target="tpu_custom_call" | custom-call | tf_op jit(solution)/shard_map/ffn/pallas_call | solution.py:260
  338.1 1.0 copy-done.13
  339.1 24.6 %ffn.6 = bf16[512,1024]{1,0:T(8,128)(2,1)} custom-call(bf16[512,1024]{1,0:T(8,128)(2,1)} %copy-done.13, f32[512,2]{1,0:T(8,128)} %get-tuple-element.25.refs_1_, bf16[4,1024,1536]{2,1,0:T(8,128)(2,1)} %bitcast.61, bf16[4,1536,1024]{2,1,0:T(8,128)(2,1)} %bitcast.65), custom_call_target="tpu_custom_call" | custom-call | tf_op jit(solution)/shard_map/ffn/pallas_call | solution.py:260
  363.7 2.5 collective-permute-start.4
  366.2 0.1 collective-permute-start.3
  366.3 24.9 %ffn.7 = f32[512,1024]{1,0:T(8,128)} custom-call(bf16[512,1024]{1,0:T(8,128)(2,1)} %copy-done.4, f32[512,2]{1,0:T(8,128)} %get-tuple-element.23.refs_1_, bf16[4,1024,1536]{2,1,0:T(8,128)(2,1)} %bitcast.62, bf16[4,1536,1024]{2,1,0:T(8,128)(2,1)} %bitcast.66), custom_call_target="tpu_custom_call" | custom-call | tf_op jit(solution)/shard_map/ffn/pallas_call | solution.py:260
  391.2 21.4 %collective-permute-done.3 = bf16[512,1024]{1,0:T(8,128)(2,1)} collective-permute-done((bf16[512,1024]{1,0:T(8,128)(2,1)S(1)}, bf16[512,1024]{1,0:T(8,128)(2,1)}, u32[]{:S(2)}, u32[]{:S(2)}) %collective-permute-start.3) | collective-permute-done | bytes 1048608 | tf_op jit(solution)/shard_map/ppermute | solution.py:211
  412.6 4.9 %fusion.6 = bf16[1024,1024]{1,0:T(8,128)(2,1)} fusion(bf16[1024,1024]{1,0:T(8,128)(2,1)} %copy-done.3, f32[512,1024]{1,0:T(8,128)} %ffn.7, f32[512,1024]{1,0:T(8,128)} %ffn.4, bf16[512,1024]{1,0:T(8,128)(2,1)} %collective-permute-done.4, bf16[512,1024]{1,0:T(8,128)(2,1)} %collective-permute-done.3), kind=kLoop, calls=%fused_computation.9 | loop fusion | flops 9437184 | bytes 10485760 | tf_op jit(solution)/shard_map/convert_element_type | solution.py:397
  (63 shorter events, 0.4 us)
Async XLA Ops:
  6.5 1.9 copy-start
  6.5 213.3 %all-gather.5.cloned.1.call-start = ((), (), s32[]{:S(2)}) async-start(), calls=%async_computation.2 | async-start | bytes 13369344 | tf_op jit(solution)/shard_map/all_gather | solution.py:306
  8.4 3.3 copy-start.16
  8.4 3.3 copy-start.17
  9.4 7.0 %copy-start.2 = (bf16[1,8,128,1024]{3,2,1,0:T(8,128)(2,1)S(1)}, bf16[1,8,128,1024]{3,2,1,0:T(8,128)(2,1)}, u32[]{:S(2)}) copy-start(bf16[1,8,128,1024]{3,2,1,0:T(8,128)(2,1)} %param.10) | copy-start | bytes 6291460
  9.4 279.2 %all-gather.7.cloned.1.call-start = ((), (), s32[]{:S(2)}) async-start(), calls=%async_computation.3 | async-start | bytes 13369344 | tf_op jit(solution)/shard_map/all_gather | solution.py:307
  12.0 19.9 %collective-permute-start = (f32[2,1024]{0,1:T(8,128)S(1)}, f32[2,1024]{0,1:T(8,128)S(1)}, u32[]{:S(2)}, u32[]{:S(2)}) collective-permute-start(f32[2,1024]{0,1:T(8,128)S(1)} %copy.22), channel_id=1, source_target_pairs={{0,4},{4,0},{1,5},{5,1},{2,6},{6,2},{3,7},{7,3},{8,12},{12,8},{9,1... | collective-permute-start | bytes 24584 | tf_op jit(solution)/shard_map/ppermute | solution.py:211
  16.7 1.5 copy-start.19
  18.2 1.4 copy-start.5
  31.9 0.8 copy-start.15
  32.8 68.9 %all-to-all-start = ((bf16[16,64,1024]{2,1,0:T(8,128)(2,1)}), bf16[16,64,1024]{2,1,0:T(8,128)(2,1)}, u32[]{:S(2)}, u32[]{:S(2)}) async-start(bf16[16,64,1024]{2,1,0:T(8,128)(2,1)} %bitcast.71), calls=%async_computation | async-start | bytes 4194304 | tf_op jit(solution)/shard_map/all_to_all | solution.py:338
  38.2 4.3 %copy-start.18 = (f32[2,1024]{1,0:T(2,128)S(1)}, f32[2,1024]{1,0:T(2,128)}, u32[]{:S(2)}) copy-start(f32[2,1024]{1,0:T(2,128)} %param.14) | copy-start | bytes 24580
  38.2 4.9 %copy-start.8 = (bf16[2,8,128,128]{3,2,1,0:T(8,128)(2,1)S(1)}, bf16[2,8,128,128]{3,2,1,0:T(8,128)(2,1)}, u32[]{:S(2)}) copy-start(bf16[2,8,128,128]{3,2,1,0:T(8,128)(2,1)} %param.12) | copy-start | bytes 1572868
  38.2 4.9 %copy-start.7 = (bf16[2,8,128,128]{3,2,1,0:T(8,128)(2,1)S(1)}, bf16[2,8,128,128]{3,2,1,0:T(8,128)(2,1)}, u32[]{:S(2)}) copy-start(bf16[2,8,128,128]{3,2,1,0:T(8,128)(2,1)} %param.13) | copy-start | bytes 1572868
  43.3 1.7 copy-start.11
  43.3 1.7 copy-start.12
  43.3 2.8 copy-start.9
  43.3 2.8 copy-start.10
  110.2 99.2 %copy-start.6 = (bf16[16,2,4,8,8,128]{5,4,3,2,1,0:T(8,128)(2,1)S(1)}, bf16[16,2,4,8,8,128]{5,4,3,2,1,0:T(8,128)(2,1)}, u32[]{:S(2)}) copy-start(bf16[16,2,4,8,8,128]{5,4,3,2,1,0:T(8,128)(2,1)} %copy-done.5) | copy-start | bytes 6291460
  212.2 1.4 copy-start.3
  212.2 0.7 copy-start.20
  214.8 98.7 %copy-start.4 = (bf16[512,1024]{1,0:T(8,128)(2,1)}, bf16[512,1024]{1,0:T(8,128)(2,1)S(1)}, u32[]{:S(2)}) copy-start(bf16[512,1024]{1,0:T(8,128)(2,1)S(1)} %get-tuple-element.16.refs_0_) | copy-start | bytes 3145732
  214.8 98.7 %collective-permute-start.1 = (bf16[512,1024]{1,0:T(8,128)(2,1)}, bf16[512,1024]{1,0:T(8,128)(2,1)}, u32[]{:S(2)}, u32[]{:S(2)}) collective-permute-start(bf16[512,1024]{1,0:T(8,128)(2,1)} %get-tuple-element.21.refs_0_), channel_id=1, source_target_pairs={{0,4},{4,0},{1,5},{5,1},{2,6},{6,2},{3,7},{7,3},{8,12},{12,8},{9,1... | collective-permute-start | bytes 3145736 | tf_op jit(solution)/shard_map/ppermute | solution.py:211
  216.8 121.3 %collective-permute-start.2 = (bf16[512,1024]{1,0:T(8,128)(2,1)S(1)}, bf16[512,1024]{1,0:T(8,128)(2,1)S(1)}, u32[]{:S(2)}, u32[]{:S(2)}) collective-permute-start(bf16[512,1024]{1,0:T(8,128)(2,1)S(1)} %get-tuple-element.16.refs_0_), channel_id=1, source_target_pairs={{0,4},{4,0},{1,5},{5,1},{2,6},{6,2},{3,7},{7,3},{8,12},{12,8},{9,1... | collective-permute-start | bytes 3145736 | tf_op jit(solution)/shard_map/ppermute | solution.py:211
  338.1 1.0 copy-start.13
  339.1 27.1 %copy-start.14 = (bf16[512,1024]{1,0:T(8,128)(2,1)S(1)}, bf16[512,1024]{1,0:T(8,128)(2,1)}, u32[]{:S(2)}) copy-start(bf16[512,1024]{1,0:T(8,128)(2,1)} %ffn.5) | copy-start | bytes 3145732
  363.7 27.5 %collective-permute-start.4 = (bf16[512,1024]{1,0:T(8,128)(2,1)}, bf16[512,1024]{1,0:T(8,128)(2,1)}, u32[]{:S(2)}, u32[]{:S(2)}) collective-permute-start(bf16[512,1024]{1,0:T(8,128)(2,1)} %ffn.6), channel_id=1, source_target_pairs={{0,4},{4,0},{1,5},{5,1},{2,6},{6,2},{3,7},{7,3},{8,12},{12,8},{9,1... | collective-permute-start | bytes 3145736 | tf_op jit(solution)/shard_map/ppermute | solution.py:211
  366.2 46.4 %collective-permute-start.3 = (bf16[512,1024]{1,0:T(8,128)(2,1)S(1)}, bf16[512,1024]{1,0:T(8,128)(2,1)}, u32[]{:S(2)}, u32[]{:S(2)}) collective-permute-start(bf16[512,1024]{1,0:T(8,128)(2,1)S(1)} %copy-done.14), channel_id=1, source_target_pairs={{0,4},{4,0},{1,5},{5,1},{2,6},{6,2},{3,7},{7,3},{8,12},{12,8},{9,1... | collective-permute-start | bytes 3145736 | tf_op jit(solution)/shard_map/ppermute | solution.py:211
  412.6 4.9 %copy-start.1 = (bf16[1,1024,1536]{2,1,0:T(8,128)(2,1)S(1)}, bf16[1,1024,1536]{2,1,0:T(8,128)(2,1)}, u32[]{:S(2)}) copy-start(bf16[1,1024,1536]{2,1,0:T(8,128)(2,1)} %param.18) | copy-start | bytes 9437188
Sparse Core Ops, SparseCore 0:
  9.6 164.3 all-gather.4
  176.3 112.3 all-gather.6

commit v3 on v2

--- a/solution.py
+++ b/solution.py
@@ -211,69 +211,66 @@
     return lax.ppermute(value, "parity", [(0, 1), (1, 0)])
 
 
-def ffn_kernel(steps, x_ref, gate_ref, up_ref, down_ref, out_ref, part_ref, total_ref):
-    expert, step = pl.program_id(0), pl.program_id(1)
-    rows = x_ref.shape[0]
-    block = min(rows, 256)
-    for start in range(0, rows, block):
-        cut = pl.ds(start, block)
-        hidden = jax.nn.gelu(
-            jnp.dot(x_ref[cut, :], up_ref[0], preferred_element_type=jnp.float32), approximate=True
-        ).astype(jnp.bfloat16)
-        out = jnp.dot(hidden, down_ref[0], preferred_element_type=jnp.float32)
-
-        @pl.when(step == 0)
-        def _():
-            part_ref[cut, :] = out
-
-        @pl.when(step > 0)
-        def _():
-            part_ref[cut, :] = part_ref[cut, :] + out
+def ffn_kernel(steps, has_base, x_ref, gate_ref, up_ref, down_ref, *rest):
+    base_ref = rest[0] if has_base else None
+    out_ref, part_ref = rest[-2:]
+    step = pl.program_id(0)
+    hidden = up_ref.shape[2]
+    wide = COLUMNS if hidden % COLUMNS == 0 else hidden
+    cuts = [pl.ds(start, wide) for start in range(0, hidden, wide)]
+
+    def lift(cut):
+        return jnp.dot(x_ref[...], up_ref[0, :, cut], preferred_element_type=jnp.float32)
+
+    out, ahead = None, lift(cuts[0])
+    for index, cut in enumerate(cuts):
+        raw = ahead
+        if index + 1 < len(cuts):
+            ahead = lift(cuts[index + 1])
+        active = jax.nn.gelu(raw, approximate=True).astype(jnp.bfloat16)
+        part = jnp.dot(active, down_ref[0, cut, :], preferred_element_type=jnp.float32)
+        out = part if out is None else out + part
+
+    @pl.when(step == 0)
+    def _():
+        part_ref[...] = out
+
+    @pl.when(step > 0)
+    def _():
+        part_ref[...] = part_ref[...] + out
 
     @pl.when(step == steps - 1)
     def _():
-        lane = lax.broadcasted_iota(jnp.int32, gate_ref.shape, 1)
-        gate = jnp.sum(jnp.where(lane == expert, gate_ref[...], 0.0), axis=1, keepdims=True)
-        add = gate * part_ref[...]
-
-        @pl.when(expert == 0)
-        def _():
-            total_ref[...] = add
-
-        @pl.when(expert > 0)
-        def _():
-            total_ref[...] = total_ref[...] + add
-
-        @pl.when(expert == pl.num_programs(0) - 1)
-        def _():
-            out_ref[...] = total_ref[...].astype(out_ref.dtype)
-
-
-def expert_ffn(rows, gates, up, down, dtype):
+        total = gate_ref[...] * part_ref[...]
+        if has_base:
+            total = total + base_ref[...]
+        out_ref[...] = total.astype(out_ref.dtype)
+
+
+COLUMNS = 512
+
+
+def expert_ffn(rows, gate, up, down, base, dtype):
     count, width = rows.shape
-    experts = gates.shape[1]
     halves, _, hidden = up.shape
-    cuts = 2
-    chunk = hidden // cuts
-    per = halves // experts
-    steps = per * cuts
+    steps = halves
+    extra = [] if base is None else [base]
+    flat = pl.BlockSpec((count, width), lambda j: (0, 0))
     return pl.pallas_call(
-        lambda *refs: ffn_kernel(steps, *refs),
-        grid=(experts, steps),
+        lambda *refs: ffn_kernel(steps, base is not None, *refs),
+        grid=(steps,),
         in_specs=[
-            pl.BlockSpec((count, width), lambda e, j: (0, 0)),
-            pl.BlockSpec((count, experts), lambda e, j: (0, 0)),
-            pl.BlockSpec((1, width, chunk), lambda e, j: (e * per + j // cuts, 0, j % cuts)),
-            pl.BlockSpec((1, chunk, width), lambda e, j: (e * per + j // cuts, j % cuts, 0)),
-        ],
-        out_specs=pl.BlockSpec((count, width), lambda e, j: (0, 0)),
+            flat,
+            pl.BlockSpec((count, 1), lambda j: (0, 0)),
+            pl.BlockSpec((1, width, hidden), lambda j: (j, 0, 0)),
+            pl.BlockSpec((1, hidden, width), lambda j: (j, 0, 0)),
+        ]
+        + [flat for _ in extra],
+        out_specs=flat,
         out_shape=jax.ShapeDtypeStruct((count, width), dtype),
-        scratch_shapes=[
-            pltpu.VMEM((count, width), jnp.float32),
-            pltpu.VMEM((count, width), jnp.float32),
-        ],
+        scratch_shapes=[pltpu.VMEM((count, width), jnp.float32)],
         name="ffn",
-    )(rows, gates, up, down)
+    )(rows, gate, up, down, *extra)
 
 
 def per_device_dense(
@@ -302,22 +299,27 @@
     down_rows = down_weight.shape[1] // copies
     up_piece = lax.dynamic_slice_in_dim(up_weight[0], share * up_rows, up_rows, 0)
     down_piece = lax.dynamic_slice_in_dim(down_weight[0], share * down_rows, down_rows, 0)
-    names = ("pair", "half", "group", "expert")
-    up_all = lax.all_gather(up_piece, names, axis=0, tiled=True)
-    down_all = lax.all_gather(down_piece, names, axis=0, tiled=True)
-    up_all = up_all.reshape((2 * pairs,) + up_weight.shape[1:])
-    down_all = down_all.reshape((2 * pairs,) + down_weight.shape[1:])
+    names = ("half", "group", "expert")
+
+    def gather(piece, whole):
+        full = lax.all_gather(piece, names, axis=0, tiled=True)
+        return full.reshape((2,) + whole.shape[1:])
+
+    def far_plane(value, hop):
+        return lax.ppermute(value, "pair", [(p, p ^ hop) for p in range(pairs)])
+
+    mine = lax.axis_index("pair")
+    held = [(gather(up_piece, up_weight), gather(down_piece, down_weight))]
 
     route = routing.reshape(n_tokens, -1)
     gate = combine.reshape(n_tokens, -1)
 
-    def gates_for(side):
-        return jnp.stack(
-            [jnp.sum(jnp.where(route == 2 * e + side, gate, 0.0), axis=1) for e in range(pairs)]
-        )
-
-    own_gates = gates_for(parity).T
-    other_gates = swap(gates_for(1 - parity))
+    def gates_for(side, hop):
+        expert = 2 * (mine ^ hop) + side
+        return jnp.sum(jnp.where(route == expert, gate, 0.0), axis=1)
+
+    own_gates = jnp.stack([gates_for(parity, hop) for hop in range(pairs)])
+    other_gates = swap(jnp.stack([gates_for(1 - parity, hop) for hop in range(pairs)]))
 
     cosine, sine = twiddle(grid_len)
     half = grid_len // 2
@@ -334,8 +336,10 @@
     col_spec = jnp.dot(columns, normed_first, preferred_element_type=jnp.float32)
     col_spec = col_spec.astype(jnp.bfloat16)
     col_spec, other_gates = lax.optimization_barrier((col_spec, other_gates))
-    other_gates = other_gates.T
     by_column = lax.all_to_all(col_spec, RING, split_axis=0, concat_axis=0, tiled=True)
+    far_up = [far_plane(up_piece, hop) for hop in range(1, pairs)]
+    by_column, far_up, down_piece = lax.optimization_barrier((by_column, far_up, down_piece))
+    far_up = [gather(piece, up_weight) for piece in far_up]
 
     none = jnp.zeros_like(cosine)
     usual = jnp.concatenate(
@@ -373,6 +377,10 @@
         1.0 / grid_len,
     )
     by_row = lax.all_to_all(row_back, RING, split_axis=0, concat_axis=0, tiled=True)
+    far_down = [far_plane(down_piece, hop) for hop in range(1, pairs)]
+    by_row, far_down = lax.optimization_barrier((by_row, far_down))
+    far_down = [gather(piece, down_weight) for piece in far_down]
+    held += list(zip(far_up, far_down))
     mixing = lax.dot_general(
         columns, by_row, (((0,), (0,)), ((), ())), preferred_element_type=jnp.float32
     ) * (1.0 / grid_len)
@@ -382,15 +390,38 @@
     step = n_tokens // 2
     near, far = normed[:step], normed[step:]
     first_in, second_in = swap(near), swap(far)
-    own_first = expert_ffn(near, own_gates[:step], up_all, down_all, jnp.float32)
-    first_in, own_first = lax.optimization_barrier((first_in, own_first))
-    first_out = expert_ffn(first_in, other_gates[:step], up_all, down_all, jnp.bfloat16)
-    first_back = swap(first_out)
-    second_in, first_out = lax.optimization_barrier((second_in, first_out))
-    second_out = expert_ffn(second_in, other_gates[step:], up_all, down_all, jnp.bfloat16)
-    second_back = swap(second_out)
-    far, second_out = lax.optimization_barrier((far, second_out))
-    own_second = expert_ffn(far, own_gates[step:], up_all, down_all, jnp.float32)
+    last = pairs - 1
+
+    def run(rows, gates, start, index, base, dtype):
+        column = gates[index, start : start + step][:, None]
+        return expert_ffn(rows, column, *held[index], base, dtype)
+
+    def after(value, other):
+        return lax.optimization_barrier((value, other))
+
+    wide = jnp.float32
+    own_first = run(near, own_gates, 0, 0, None, wide)
+    far, own_first = after(far, own_first)
+    own_second = run(far, own_gates, step, 0, None, wide)
+    first_in, own_second = after(first_in, own_second)
+    first_out = run(first_in, other_gates, 0, 0, None, wide)
+    second_in, first_out = after(second_in, first_out)
+    second_out = run(second_in, other_gates, step, 0, None, wide)
+    for index in range(1, pairs):
+        kind = jnp.bfloat16 if index == last else wide
+        first_in, second_out = after(first_in, second_out)
+        first_out = run(first_in, other_gates, 0, index, first_out, kind)
+        if index == last:
+            first_back = swap(first_out)
+        second_in, first_out = after(second_in, first_out)
+        second_out = run(second_in, other_gates, step, index, second_out, kind)
+        if index == last:
+            second_back = swap(second_out)
+        near, second_out = after(near, second_out)
+        own_first = run(near, own_gates, 0, index, own_first, wide)
+        far, own_first = after(far, own_first)
+        own_second = run(far, own_gates, step, index, own_second, wide)
+        first_in, own_second = after(first_in, own_second)
     own = jnp.concatenate([own_first, own_second], axis=0)
     back = jnp.concatenate([first_back, second_back], axis=0)
     final = residual.astype(jnp.float32) + own + back.astype(jnp.float32)

time: 425 us -> 370 us (0.87); the launches traced: 424 us -> 363 us
  blocking collectives: 99.2 us -> 0 us
  waiting for transfers between devices: 153 us -> 178 us
  starting transfers between devices: 13.2 us -> 22.8 us
    ppermute x0 -> x2, waiting for transfers between devices: none -> 157 us  [far_plane(): return lax.ppermute(value, 'pair', [(p, p ^ hop) for p in range(pairs)])]
    all_to_all x1 -> x0, blocking collectives: 99.2 us -> none  [per_device_dense(): lax.all_to_all(row_back, RING, split_axis=0, concat_axis=0, tiled=True)]
    all_gather x2 -> x4, waiting for transfers between devices: 68.8 us -> 0.01 us  [gather(): full = lax.all_gather(piece, names, axis=0, tiled=True)]
    all_to_all x1, waiting for transfers between devices: 54.4 us -> 0.01 us  [per_device_dense(): lax.all_to_all(col_spec, RING, split_axis=0, concat_axis=0, tiled=True)]
    ppermute x5, waiting for transfers between devices: 30.1 us -> 20.3 us  [swap(): return lax.ppermute(value, 'parity', [(0, 1), (1, 0)])]
    another operation x2 -> x11, local copies, waits for them, and re-layouts: 0.44 us -> 6.92 us  [run(): column = gates[index, start:start + step][:, None]]
    ppermute x0 -> x2, starting transfers between devices: none -> 5.59 us  [far_plane(): return lax.ppermute(value, 'pair', [(p, p ^ hop) for p in range(pairs)])]
    all_to_all x0 -> x1, starting transfers between devices: none -> 4.75 us  [per_device_dense(): lax.all_to_all(row_back, RING, split_axis=0, concat_axis=0, tiled=True)]
  transfers between devices with their start and end apart: 8 -> 13, of which waited for: 4 -> 4; matrix products, arithmetic and copies ran while one was open for 6% -> 9% of each run, Pallas kernels for 20% -> 23%
where the time goes in v3:
time: 370 us; the launch traced here: 363 us
  waiting for transfers between devices  178 us (48%)
  Pallas kernels  107 us (29%)
  starting transfers between devices  22.8 us (6%)
  local copies, waits for them, and re-layouts  17.2 us (5%)
  other arithmetic  16.1 us (4%)
  between operations  14 us (4%)
  matrix products  8.62 us (2%)
    ppermute x2, waiting for transfers between devices, far_plane(): return lax.ppermute(value, 'pair', [(p, p ^ hop) for p in range(pairs)])  157 us
    pallas_call x8, Pallas kernels, expert_ffn(): pl.pallas_call(lambda *refs: ffn_kernel(steps, base is not None, *refs),...  98.2 us
    ppermute x5, waiting for transfers between devices, swap(): return lax.ppermute(value, 'parity', [(0, 1), (1, 0)])  20.3 us
    pallas_call x1, Pallas kernels, mixer(): pl.pallas_call(body, grid=(nblocks // per_step,), in_specs=[pl.BlockSpec(...  8.46 us
  transfers between devices with their start and end apart: 13, of which 4 were waited for; matrix products, arithmetic and copies ran while one was open for 9% of the time, Pallas kernels for 23%

profile of v3, /device:TPU:0, one launch (start us, length us, event | category | flops | bytes accessed | tf_op | source)
XLA Modules:
  0.0 363.3 jit_solution(7766034541774207415)
XLA Ops:
  6.5 1.9 copy-done
  8.4 1.0 constant_dynamic-slice_fusion.1
  9.5 2.1 constant_dynamic-slice_fusion
  11.7 3.1 collective-permute-start
  15.5 1.9 convert_reduce_fusion.1
  17.4 0.7 multiply_reduce_fusion
  18.2 0.7 broadcast_multiply_fusion
  18.9 0.7 multiply_convert_fusion
  19.6 0.7 copy-done.8
  20.3 3.7 %fusion.11 = bf16[1024,1024]{1,0:T(8,128)(2,1)} fusion(bf16[1024,1024]{1,0:T(8,128)(2,1)S(1)} %bitcast.96, bf16[128,8,8,128]{3,2,1,0:T(8,128)(2,1)S(1)} %bitcast.97), kind=kOutput, calls=%fused_computation.20 | convolution fusion | flops 2148532224 | bytes 6291456 | tf_op jit(solution)/shard_map/dot_general | solution.py:336
  23.9 5.0 %all-to-all-start = ((bf16[16,64,1024]{2,1,0:T(8,128)(2,1)}), bf16[16,64,1024]{2,1,0:T(8,128)(2,1)}, u32[]{:S(2)}, u32[]{:S(2)}) async-start(bf16[16,64,1024]{2,1,0:T(8,128)(2,1)} %bitcast.99), calls=%async_computation | async-start | bytes 4194304 | tf_op jit(solution)/shard_map/all_to_all | solution.py:339
  29.1 2.8 collective-permute-start.1
  31.9 2.1 fusion.36
  34.0 77.7 %collective-permute-done.1 = bf16[256,1536]{1,0:T(8,128)(2,1)S(1)} collective-permute-done((bf16[256,1536]{1,0:T(8,128)(2,1)S(1)}, bf16[256,1536]{1,0:T(8,128)(2,1)S(1)}, u32[]{:S(2)}, u32[]{:S(2)}) %collective-permute-start.1) | collective-permute-done | bytes 786464 | tf_op jit(solution)/shard_map/ppermute | solution.py:309
  111.7 0.9 copy-done.12
  113.3 0.6 pad_maximum_fusion.1.refs_5_
  114.1 1.7 maximum_maximum_fusion
  115.8 1.2 select_convert_fusion.refs_2_
  117.0 1.2 select_convert_fusion.1.refs_1_
  118.2 8.5 %mixer.1 = bf16[1024,1024]{1,0:T(8,128)(2,1)} custom-call(bf16[1024,1024]{1,0:T(8,128)(2,1)} %bitcast.9.refs_0_, bf16[4,512,256]{2,1,0:T(8,128)(2,1)} %select_convert_fusion.1.refs_1_, bf16[4,256,512]{2,1,0:T(8,128)(2,1)} %select_convert_fusion.refs_2_, bf16[8,256,256]{2,1,0:T(8,128)(2,1)} %get-tuple-element.73.refs_3_, ...), custom_call_target="tpu_custom_call" | custom-call | tf_op jit(solution)/shard_map/mixer/pallas_call | solution.py:187
  126.6 4.7 %all-to-all-start.1 = ((bf16[16,64,1024]{2,1,0:T(8,128)(2,1)}), bf16[16,64,1024]{2,1,0:T(8,128)(2,1)}, u32[]{:S(2)}, u32[]{:S(2)}) async-start(bf16[16,64,1024]{2,1,0:T(8,128)(2,1)} %bitcast.95), calls=%async_computation.1 | async-start | bytes 4194304 | tf_op jit(solution)/shard_map/all_to_all | solution.py:379
  131.6 2.8 collective-permute-start.2
  134.4 79.8 %collective-permute-done.2 = bf16[384,1024]{1,0:T(8,128)(2,1)} collective-permute-done((bf16[384,1024]{1,0:T(8,128)(2,1)S(1)}, bf16[384,1024]{1,0:T(8,128)(2,1)}, u32[]{:S(2)}, u32[]{:S(2)}) %collective-permute-start.2) | collective-permute-done | bytes 786464 | tf_op jit(solution)/shard_map/ppermute | solution.py:309
  214.2 5.0 %convert_reduce_fusion = (f32[1024]{0:T(1024)S(1)}, bf16[1024,1024]{1,0:T(8,128)(2,1)S(1)}) fusion(bf16[1024,1024]{1,0:T(8,128)(2,1)} %bitcast.21, bf16[128,8,8,128]{3,2,1,0:T(8,128)(2,1)} %bitcast.98, bf16[1,8,128,1024]{3,2,1,0:T(8,128)(2,1)S(1)} %copy-done.3), kind=kOutput, calls=%fused_computation.2 | convolution fusion | flops 2153774080 | bytes 8392704 | tf_op jit(solution)/shard_map/dot_general | solution.py:384
  219.2 0.7 fusion.2
  219.9 0.7 fusion.4
  220.9 2.0 collective-permute-start.3
  222.9 0.9 copy.17.refs_1_
  223.8 0.9 copy.18.refs_1_
  224.6 0.8 copy.19.refs_1_
  225.5 0.9 copy.20.refs_1_
  226.3 0.9 copy.21.refs_1_
  227.2 0.9 copy.22.refs_1_
  228.1 11.9 %ffn.8.refs_4_ = f32[512,1024]{1,0:T(8,128)} custom-call(bf16[512,1024]{1,0:T(8,128)(2,1)} %copy-done.6, f32[512,1]{1,0:T(8,128)} %copy.17.refs_1_, bf16[2,1024,1536]{2,1,0:T(8,128)(2,1)} %bitcast.87, bf16[2,1536,1024]{2,1,0:T(8,128)(2,1)} %bitcast.91), custom_call_target="tpu_custom_call" | custom-call | tf_op jit(solution)/shard_map/ffn/pallas_call | solution.py:259
  240.0 11.9 %ffn.9.refs_4_ = f32[512,1024]{1,0:T(8,128)} custom-call(bf16[512,1024]{1,0:T(8,128)(2,1)} %copy-done.5, f32[512,1]{1,0:T(8,128)} %copy.18.refs_1_, bf16[2,1024,1536]{2,1,0:T(8,128)(2,1)} %bitcast.88, bf16[2,1536,1024]{2,1,0:T(8,128)(2,1)} %bitcast.92), custom_call_target="tpu_custom_call" | custom-call | tf_op jit(solution)/shard_map/ffn/pallas_call | solution.py:259
  252.0 1.0 copy-done.7
  252.9 12.0 %ffn.10.refs_4_ = f32[512,1024]{1,0:T(8,128)} custom-call(bf16[512,1024]{1,0:T(8,128)(2,1)} %copy-done.7, f32[512,1]{1,0:T(8,128)} %copy.19.refs_1_, bf16[2,1024,1536]{2,1,0:T(8,128)(2,1)} %bitcast.89, bf16[2,1536,1024]{2,1,0:T(8,128)(2,1)} %bitcast.93), custom_call_target="tpu_custom_call" | custom-call | tf_op jit(solution)/shard_map/ffn/pallas_call | solution.py:259
  264.9 3.1 collective-permute-done.3.refs_0_
  268.0 12.1 %ffn.11.refs_4_ = f32[512,1024]{1,0:T(8,128)} custom-call(bf16[512,1024]{1,0:T(8,128)(2,1)} %collective-permute-done.3.refs_0_, f32[512,1]{1,0:T(8,128)} %copy.20.refs_1_, bf16[2,1024,1536]{2,1,0:T(8,128)(2,1)} %bitcast.90, bf16[2,1536,1024]{2,1,0:T(8,128)(2,1)} %bitcast.94), custom_call_target="tpu_custom_call" | custom-call | tf_op jit(solution)/shard_map/ffn/pallas_call | solution.py:259
  280.1 12.3 %ffn.12 = bf16[512,1024]{1,0:T(8,128)(2,1)} custom-call(bf16[512,1024]{1,0:T(8,128)(2,1)} %copy-done.7, f32[512,1]{1,0:T(8,128)} %copy.21.refs_1_, bf16[2,1024,1536]{2,1,0:T(8,128)(2,1)} %bitcast.79, bf16[2,1536,1024]{2,1,0:T(8,128)(2,1)} %bitcast.83, f32[512,1024]{1,0:T(8,128)} %ffn.10.refs_4_), custom_call_target="tpu_custom_call" | custom-call | tf_op jit(solution)/shard_map/ffn/pallas_call | solution.py:259
  292.4 12.4 %ffn.13 = bf16[512,1024]{1,0:T(8,128)(2,1)} custom-call(bf16[512,1024]{1,0:T(8,128)(2,1)} %collective-permute-done.3.refs_0_, f32[512,1]{1,0:T(8,128)} %copy.22.refs_1_, bf16[2,1024,1536]{2,1,0:T(8,128)(2,1)} %bitcast.80, bf16[2,1536,1024]{2,1,0:T(8,128)(2,1)} %bitcast.84, f32[512,1024]{1,0:T(8,128)} %ffn.11.refs_4_), custom_call_target="tpu_custom_call" | custom-call | tf_op jit(solution)/shard_map/ffn/pallas_call | solution.py:259
  305.1 1.7 collective-permute-start.5
  306.9 0.9 copy.23.refs_1_
  307.8 0.9 copy.24.refs_1_
  308.6 12.9 %ffn.14 = f32[512,1024]{1,0:T(8,128)} custom-call(bf16[512,1024]{1,0:T(8,128)(2,1)} %copy-done.6, f32[512,1]{1,0:T(8,128)} %copy.23.refs_1_, bf16[2,1024,1536]{2,1,0:T(8,128)(2,1)} %bitcast.81, bf16[2,1536,1024]{2,1,0:T(8,128)(2,1)} %bitcast.85, f32[512,1024]{1,0:T(8,128)} %ffn.8.refs_4_), custom_call_target="tpu_custom_call" | custom-call | tf_op jit(solution)/shard_map/ffn/pallas_call | solution.py:259
  321.5 12.7 %ffn.15 = f32[512,1024]{1,0:T(8,128)} custom-call(bf16[512,1024]{1,0:T(8,128)(2,1)} %copy-done.5, f32[512,1]{1,0:T(8,128)} %copy.24.refs_1_, bf16[2,1024,1536]{2,1,0:T(8,128)(2,1)} %bitcast.82, bf16[2,1536,1024]{2,1,0:T(8,128)(2,1)} %bitcast.86, f32[512,1024]{1,0:T(8,128)} %ffn.9.refs_4_), custom_call_target="tpu_custom_call" | custom-call | tf_op jit(solution)/shard_map/ffn/pallas_call | solution.py:259
  334.2 17.2 %collective-permute-done.5 = bf16[512,1024]{1,0:T(8,128)(2,1)} collective-permute-done((bf16[512,1024]{1,0:T(8,128)(2,1)S(1)}, bf16[512,1024]{1,0:T(8,128)(2,1)}, u32[]{:S(2)}, u32[]{:S(2)}) %collective-permute-start.5) | collective-permute-done | bytes 1048608 | tf_op jit(solution)/shard_map/ppermute | solution.py:211
  351.4 4.9 %fusion.6 = bf16[1024,1024]{1,0:T(8,128)(2,1)} fusion(bf16[1024,1024]{1,0:T(8,128)(2,1)} %copy-done.4, f32[512,1024]{1,0:T(8,128)} %ffn.15, f32[512,1024]{1,0:T(8,128)} %ffn.14, bf16[512,1024]{1,0:T(8,128)(2,1)} %collective-permute-done.6, bf16[512,1024]{1,0:T(8,128)(2,1)} %collective-permute-done.5), kind=kLoop, calls=%fused_computation.9 | loop fusion | flops 9437184 | bytes 10485760 | tf_op jit(solution)/shard_map/convert_element_type | solution.py:428
  (82 shorter events, 2.6 us)
Async XLA Ops:
  6.5 1.9 copy-start
  6.5 221.5 %all-gather.11.cloned.1.call-start = ((), (), s32[]{:S(2)}) async-start(), calls=%async_computation.4 | async-start | bytes 7077888 | tf_op jit(solution)/shard_map/all_gather | solution.py:305
  8.4 3.2 copy-start.14
  8.4 3.2 copy-start.15
  9.4 218.7 %all-gather.13.cloned.1.call-start = ((), (), s32[]{:S(2)}) async-start(), calls=%async_computation.5 | async-start | bytes 7077888 | tf_op jit(solution)/shard_map/all_gather | solution.py:305
  11.6 5.8 %copy-start.2 = (bf16[1,8,128,1024]{3,2,1,0:T(8,128)(2,1)S(1)}, bf16[1,8,128,1024]{3,2,1,0:T(8,128)(2,1)}, u32[]{:S(2)}) copy-start(bf16[1,8,128,1024]{3,2,1,0:T(8,128)(2,1)} %param.10) | copy-start | bytes 6291460
  11.7 12.2 %collective-permute-start = (f32[2,1024]{1,0:T(2,128)S(1)}, f32[2,1024]{1,0:T(2,128)S(1)}, u32[]{:S(2)}, u32[]{:S(2)}) collective-permute-start(f32[2,1024]{1,0:T(2,128)S(1)} %pad_maximum_fusion), channel_id=1, source_target_pairs={{0,4},{4,0},{1,5},{5,1},{2,6},{6,2},{3,7},{7,3},{8,12},{12,8},{9,1... | collective-permute-start | bytes 24584 | tf_op jit(solution)/shard_map/ppermute | solution.py:211
  17.4 1.5 copy-start.17
  18.9 1.4 copy-start.8
  23.9 87.7 %all-to-all-start = ((bf16[16,64,1024]{2,1,0:T(8,128)(2,1)}), bf16[16,64,1024]{2,1,0:T(8,128)(2,1)}, u32[]{:S(2)}, u32[]{:S(2)}) async-start(bf16[16,64,1024]{2,1,0:T(8,128)(2,1)} %bitcast.99), calls=%async_computation | async-start | bytes 4194304 | tf_op jit(solution)/shard_map/all_to_all | solution.py:339
  28.9 251.2 %all-gather.7.cloned.1.call-start = ((), (), s32[]{:S(2)}) async-start(), calls=%async_computation.2 | async-start | bytes 7077888 | tf_op jit(solution)/shard_map/all_gather | solution.py:305
  29.1 84.3 %copy-start.16 = (f32[2,1024]{1,0:T(2,128)S(1)}, f32[2,1024]{1,0:T(2,128)}, u32[]{:S(2)}) copy-start(f32[2,1024]{1,0:T(2,128)} %param.14) | copy-start | bytes 24580
  29.1 84.9 %copy-start.10 = (bf16[2,8,128,128]{3,2,1,0:T(8,128)(2,1)S(1)}, bf16[2,8,128,128]{3,2,1,0:T(8,128)(2,1)}, u32[]{:S(2)}) copy-start(bf16[2,8,128,128]{3,2,1,0:T(8,128)(2,1)} %param.12) | copy-start | bytes 1572868
  29.1 82.6 %collective-permute-start.1 = (bf16[256,1536]{1,0:T(8,128)(2,1)S(1)}, bf16[256,1536]{1,0:T(8,128)(2,1)S(1)}, u32[]{:S(2)}, u32[]{:S(2)}) collective-permute-start(bf16[256,1536]{1,0:T(8,128)(2,1)S(1)} %fusion.37), channel_id=1, source_target_pairs={{0,8},{8,0},{1,9},{9,1},{2,10},{10,2},{3,11},{11,3},{4,12},{12,4},... | collective-permute-start | bytes 2359304 | tf_op jit(solution)/shard_map/ppermute | solution.py:309
  34.0 80.0 %copy-start.9 = (bf16[2,8,128,128]{3,2,1,0:T(8,128)(2,1)S(1)}, bf16[2,8,128,128]{3,2,1,0:T(8,128)(2,1)}, u32[]{:S(2)}) copy-start(bf16[2,8,128,128]{3,2,1,0:T(8,128)(2,1)} %param.13) | copy-start | bytes 1572868
  111.7 0.9 copy-start.12
  126.6 5.0 %copy-start.13 = (bf16[384,1024]{1,0:T(8,128)(2,1)S(1)}, bf16[384,1024]{1,0:T(8,128)(2,1)}, u32[]{:S(2)}) copy-start(bf16[384,1024]{1,0:T(8,128)(2,1)} %fusion.36) | copy-start | bytes 2359300
  126.6 87.5 %copy-start.3 = (bf16[1,8,128,1024]{3,2,1,0:T(8,128)(2,1)S(1)}, bf16[1,8,128,1024]{3,2,1,0:T(8,128)(2,1)}, u32[]{:S(2)}) copy-start(bf16[1,8,128,1024]{3,2,1,0:T(8,128)(2,1)} %param.10) | copy-start | bytes 6291460
  126.6 87.5 %all-to-all-start.1 = ((bf16[16,64,1024]{2,1,0:T(8,128)(2,1)}), bf16[16,64,1024]{2,1,0:T(8,128)(2,1)}, u32[]{:S(2)}, u32[]{:S(2)}) async-start(bf16[16,64,1024]{2,1,0:T(8,128)(2,1)} %bitcast.95), calls=%async_computation.1 | async-start | bytes 4194304 | tf_op jit(solution)/shard_map/all_to_all | solution.py:379
  131.4 148.7 %all-gather.9.cloned.1.call-start = ((), (), s32[]{:S(2)}) async-start(), calls=%async_computation.3 | async-start | bytes 7077888 | tf_op jit(solution)/shard_map/all_gather | solution.py:305
  131.6 82.5 %collective-permute-start.2 = (bf16[384,1024]{1,0:T(8,128)(2,1)S(1)}, bf16[384,1024]{1,0:T(8,128)(2,1)}, u32[]{:S(2)}, u32[]{:S(2)}) collective-permute-start(bf16[384,1024]{1,0:T(8,128)(2,1)S(1)} %copy-done.13), channel_id=1, source_target_pairs={{0,8},{8,0},{1,9},{9,1},{2,10},{10,2},{3,11},{11,3},{4,12},{12,4},... | collective-permute-start | bytes 2359304 | tf_op jit(solution)/shard_map/ppermute | solution.py:309
  219.1 1.4 copy-start.4
  219.1 0.7 copy-start.18
  220.8 7.3 %copy-start.6 = (bf16[512,1024]{1,0:T(8,128)(2,1)}, bf16[512,1024]{1,0:T(8,128)(2,1)S(1)}, u32[]{:S(2)}) copy-start(bf16[512,1024]{1,0:T(8,128)(2,1)S(1)} %get-tuple-element.39.refs_0_) | copy-start | bytes 3145732
  220.8 19.2 %copy-start.5 = (bf16[512,1024]{1,0:T(8,128)(2,1)}, bf16[512,1024]{1,0:T(8,128)(2,1)S(1)}, u32[]{:S(2)}) copy-start(bf16[512,1024]{1,0:T(8,128)(2,1)S(1)} %get-tuple-element.42.refs_0_) | copy-start | bytes 3145732
  220.8 31.2 %collective-permute-start.4 = (bf16[512,1024]{1,0:T(8,128)(2,1)S(1)}, bf16[512,1024]{1,0:T(8,128)(2,1)S(1)}, u32[]{:S(2)}, u32[]{:S(2)}) collective-permute-start(bf16[512,1024]{1,0:T(8,128)(2,1)S(1)} %get-tuple-element.39.refs_0_), channel_id=1, source_target_pairs={{0,4},{4,0},{1,5},{5,1},{2,6},{6,2},{3,7},{7,3},{8,12},{12,8},{9,1... | collective-permute-start | bytes 3145736 | tf_op jit(solution)/shard_map/ppermute | solution.py:211
  220.9 47.2 %collective-permute-start.3 = (bf16[512,1024]{1,0:T(8,128)(2,1)S(1)}, bf16[512,1024]{1,0:T(8,128)(2,1)}, u32[]{:S(2)}, u32[]{:S(2)}) collective-permute-start(bf16[512,1024]{1,0:T(8,128)(2,1)S(1)} %get-tuple-element.42.refs_0_), channel_id=1, source_target_pairs={{0,4},{4,0},{1,5},{5,1},{2,6},{6,2},{3,7},{7,3},{8,12},{12,8},{9,1... | collective-permute-start | bytes 3145736 | tf_op jit(solution)/shard_map/ppermute | solution.py:211
  251.9 1.0 copy-start.7
  292.4 12.7 %copy-start.11 = (bf16[512,1024]{1,0:T(8,128)(2,1)S(1)}, bf16[512,1024]{1,0:T(8,128)(2,1)}, u32[]{:S(2)}) copy-start(bf16[512,1024]{1,0:T(8,128)(2,1)} %ffn.12) | copy-start | bytes 3145732
  304.9 29.3 %collective-permute-start.6 = (bf16[512,1024]{1,0:T(8,128)(2,1)}, bf16[512,1024]{1,0:T(8,128)(2,1)}, u32[]{:S(2)}, u32[]{:S(2)}) collective-permute-start(bf16[512,1024]{1,0:T(8,128)(2,1)} %ffn.13), channel_id=1, source_target_pairs={{0,4},{4,0},{1,5},{5,1},{2,6},{6,2},{3,7},{7,3},{8,12},{12,8},{9,1... | collective-permute-start | bytes 3145736 | tf_op jit(solution)/shard_map/ppermute | solution.py:211
  305.1 46.2 %collective-permute-start.5 = (bf16[512,1024]{1,0:T(8,128)(2,1)S(1)}, bf16[512,1024]{1,0:T(8,128)(2,1)}, u32[]{:S(2)}, u32[]{:S(2)}) collective-permute-start(bf16[512,1024]{1,0:T(8,128)(2,1)S(1)} %copy-done.11), channel_id=1, source_target_pairs={{0,4},{4,0},{1,5},{5,1},{2,6},{6,2},{3,7},{7,3},{8,12},{12,8},{9,1... | collective-permute-start | bytes 3145736 | tf_op jit(solution)/shard_map/ppermute | solution.py:211
  351.4 4.9 %copy-start.1 = (bf16[1,1024,1536]{2,1,0:T(8,128)(2,1)S(1)}, bf16[1,1024,1536]{2,1,0:T(8,128)(2,1)}, u32[]{:S(2)}) copy-start(bf16[1,1024,1536]{2,1,0:T(8,128)(2,1)} %param.18) | copy-start | bytes 9437188
Sparse Core Ops, SparseCore 0:
  9.5 61.9 all-gather.10
  73.4 46.9 all-gather.12
  122.3 66.2 all-gather.6
  214.3 44.3 all-gather.8

commit v4 on v3

--- a/solution.py
+++ b/solution.py
@@ -214,7 +214,7 @@
 def ffn_kernel(steps, has_base, x_ref, gate_ref, up_ref, down_ref, *rest):
     base_ref = rest[0] if has_base else None
     out_ref, part_ref = rest[-2:]
-    step = pl.program_id(0)
+    step = pl.program_id(1)
     hidden = up_ref.shape[2]
     wide = COLUMNS if hidden % COLUMNS == 0 else hidden
     cuts = [pl.ds(start, wide) for start in range(0, hidden, wide)]
@@ -250,25 +250,24 @@
 COLUMNS = 512
 
 
-def expert_ffn(rows, gate, up, down, base, dtype):
+def expert_ffn(rows, gate, up, down, base, block, dtype):
     count, width = rows.shape
-    halves, _, hidden = up.shape
-    steps = halves
+    steps, _, hidden = up.shape
     extra = [] if base is None else [base]
-    flat = pl.BlockSpec((count, width), lambda j: (0, 0))
+    flat = pl.BlockSpec((block, width), lambda i, j: (i, 0))
     return pl.pallas_call(
         lambda *refs: ffn_kernel(steps, base is not None, *refs),
-        grid=(steps,),
+        grid=(count // block, steps),
         in_specs=[
             flat,
-            pl.BlockSpec((count, 1), lambda j: (0, 0)),
-            pl.BlockSpec((1, width, hidden), lambda j: (j, 0, 0)),
-            pl.BlockSpec((1, hidden, width), lambda j: (j, 0, 0)),
+            pl.BlockSpec((block, 1), lambda i, j: (i, 0)),
+            pl.BlockSpec((1, width, hidden), lambda i, j: (j, 0, 0)),
+            pl.BlockSpec((1, hidden, width), lambda i, j: (j, 0, 0)),
         ]
         + [flat for _ in extra],
         out_specs=flat,
         out_shape=jax.ShapeDtypeStruct((count, width), dtype),
-        scratch_shapes=[pltpu.VMEM((count, width), jnp.float32)],
+        scratch_shapes=[pltpu.VMEM((block, width), jnp.float32)],
         name="ffn",
     )(rows, gate, up, down, *extra)
 
@@ -335,12 +334,6 @@
     normed_first = layer_norm(tokens, ln_first).astype(jnp.bfloat16).reshape(n_tokens, width)
     col_spec = jnp.dot(columns, normed_first, preferred_element_type=jnp.float32)
     col_spec = col_spec.astype(jnp.bfloat16)
-    col_spec, other_gates = lax.optimization_barrier((col_spec, other_gates))
-    by_column = lax.all_to_all(col_spec, RING, split_axis=0, concat_axis=0, tiled=True)
-    far_up = [far_plane(up_piece, hop) for hop in range(1, pairs)]
-    by_column, far_up, down_piece = lax.optimization_barrier((by_column, far_up, down_piece))
-    far_up = [gather(piece, up_weight) for piece in far_up]
-
     none = jnp.zeros_like(cosine)
     usual = jnp.concatenate(
         [
@@ -366,16 +359,20 @@
     bias = jnp.concatenate(
         [spec_bias[0].reshape(nblocks, 1, bwidth), spec_bias[1].reshape(nblocks, 1, bwidth)], axis=2
     )
-    row_back = mixer(
-        by_column,
+    prepared = (
         rows_matrix,
         rows_matrix.transpose(0, 2, 1),
         complex_square(spec_first),
         complex_square(spec_second),
         bias,
-        slots,
-        1.0 / grid_len,
-    )
+    )
+    col_spec, other_gates, prepared = lax.optimization_barrier((col_spec, other_gates, prepared))
+    by_column = lax.all_to_all(col_spec, RING, split_axis=0, concat_axis=0, tiled=True)
+    far_up = [far_plane(up_piece, hop) for hop in range(1, pairs)]
+    by_column, far_up, down_piece = lax.optimization_barrier((by_column, far_up, down_piece))
+    far_up = [gather(piece, up_weight) for piece in far_up]
+
+    row_back = mixer(by_column, *prepared, slots, 1.0 / grid_len)
     by_row = lax.all_to_all(row_back, RING, split_axis=0, concat_axis=0, tiled=True)
     far_down = [far_plane(down_piece, hop) for hop in range(1, pairs)]
     by_row, far_down = lax.optimization_barrier((by_row, far_down))
@@ -392,37 +389,32 @@
     first_in, second_in = swap(near), swap(far)
     last = pairs - 1
 
-    def run(rows, gates, start, index, base, dtype):
-        column = gates[index, start : start + step][:, None]
-        return expert_ffn(rows, column, *held[index], base, dtype)
+    def run(rows, gates, index, base, dtype):
+        return expert_ffn(rows, gates[index][:, None], *held[index], base, step, dtype)
 
     def after(value, other):
         return lax.optimization_barrier((value, other))
 
     wide = jnp.float32
-    own_first = run(near, own_gates, 0, 0, None, wide)
-    far, own_first = after(far, own_first)
-    own_second = run(far, own_gates, step, 0, None, wide)
-    first_in, own_second = after(first_in, own_second)
-    first_out = run(first_in, other_gates, 0, 0, None, wide)
+    near_gates, far_gates = other_gates[:, :step], other_gates[:, step:]
+    own = run(normed, own_gates, 0, None, wide)
+    first_in, own = after(first_in, own)
+    first_out = run(first_in, near_gates, 0, None, wide)
     second_in, first_out = after(second_in, first_out)
-    second_out = run(second_in, other_gates, step, 0, None, wide)
+    second_out = run(second_in, far_gates, 0, None, wide)
     for index in range(1, pairs):
         kind = jnp.bfloat16 if index == last else wide
         first_in, second_out = after(first_in, second_out)
-        first_out = run(first_in, other_gates, 0, index, first_out, kind)
+        first_out = run(first_in, near_gates, index, first_out, kind)
         if index == last:
             first_back = swap(first_out)
         second_in, first_out = after(second_in, first_out)
-        second_out = run(second_in, other_gates, step, index, second_out, kind)
+        second_out = run(second_in, far_gates, index, second_out, kind)
         if index == last:
             second_back = swap(second_out)
-        near, second_out = after(near, second_out)
-        own_first = run(near, own_gates, 0, index, own_first, wide)
-        far, own_first = after(far, own_first)
-        own_second = run(far, own_gates, step, index, own_second, wide)
-        first_in, own_second = after(first_in, own_second)
-    own = jnp.concatenate([own_first, own_second], axis=0)
+        normed, second_out = after(normed, second_out)
+        own = run(normed, own_gates, index, own, wide)
+        first_in, own = after(first_in, own)
     back = jnp.concatenate([first_back, second_back], axis=0)
     final = residual.astype(jnp.float32) + own + back.astype(jnp.float32)
     return final.reshape(tokens.shape).astype(jnp.bfloat16)
@@ -431,6 +423,7 @@
 def solution(mesh):
     shape = mesh.shape
     group, row, expert = shape["group"], shape["row"], shape["expert"]
+
     def placed(row_names):
         cells = P("group", row_names + ("expert",), None, None)
         weights = P(row_names, None, None)
@@ -449,6 +442,7 @@
                 ("group", "pair", "parity", "half", "expert"),
             )
             ins, outs = placed(("pair", "parity", "half"))
+
             call = jax.shard_map(
                 per_device_dense, mesh=split, in_specs=ins, out_specs=outs, check_vma=False
             )

time: 370 us -> 374 us (1.011); the launches traced: 363 us -> 373 us
  waiting for transfers between devices: 178 us -> 188 us
  Pallas kernels: 107 us -> 97.5 us
  local copies, waits for them, and re-layouts: 17.2 us -> 23 us
  other arithmetic: 16.1 us -> 20.2 us
    ppermute x5, waiting for transfers between devices: 20.3 us -> 30.2 us  [swap(): return lax.ppermute(value, 'parity', [(0, 1), (1, 0)])]
    pallas_call x8 -> x6, Pallas kernels: 98.2 us -> 89.1 us  [expert_ffn(): pl.pallas_call(lambda *refs: ffn_kernel(steps, base is not None, *refs),...]
  transfers between devices with their start and end apart: 13 -> 13, of which waited for: 4 -> 5; matrix products, arithmetic and copies ran while one was open for 9% -> 10% of each run, Pallas kernels for 23% -> 19%
where the time goes in v4:
time: 374 us; the launch traced here: 373 us
  waiting for transfers between devices  188 us (50%)
  Pallas kernels  97.5 us (26%)
  local copies, waits for them, and re-layouts  23 us (6%)
  starting transfers between devices  22.6 us (6%)
  other arithmetic  20.2 us (5%)
  between operations  13.5 us (4%)
  matrix products  8.62 us (2%)
    ppermute x2, waiting for transfers between devices, far_plane(): return lax.ppermute(value, 'pair', [(p, p ^ hop) for p in range(pairs)])  157 us
    pallas_call x6, Pallas kernels, expert_ffn(): pl.pallas_call(lambda *refs: ffn_kernel(steps, base is not None, *refs),...  89.1 us
    ppermute x5, waiting for transfers between devices, swap(): return lax.ppermute(value, 'parity', [(0, 1), (1, 0)])  30.2 us
    pallas_call x1, Pallas kernels, mixer(): pl.pallas_call(body, grid=(nblocks // per_step,), in_specs=[pl.BlockSpec(...  8.42 us
  transfers between devices with their start and end apart: 13, of which 5 were waited for; matrix products, arithmetic and copies ran while one was open for 10% of the time, Pallas kernels for 19%

profile of v4, /device:TPU:0, one launch (start us, length us, event | category | flops | bytes accessed | tf_op | source)
XLA Modules:
  0.0 373.0 jit_solution(18057212754198362151)
XLA Ops:
  6.5 1.9 copy-done
  8.4 1.0 constant_dynamic-slice_fusion.1
  9.5 2.1 constant_dynamic-slice_fusion
  12.9 3.1 collective-permute-start
  16.8 0.7 fusion.31
  17.5 0.8 copy.16
  18.4 0.8 fusion.32
  19.1 0.8 copy.15
  20.0 1.1 fusion.29
  21.1 1.0 fusion.30
  22.1 1.1 slice_bitcast_fusion
  23.2 1.7 maximum_maximum_fusion
  26.8 1.1 select_convert_fusion.refs_2_
  27.9 1.2 select_convert_fusion.1.refs_1_
  31.2 3.7 fusion.11
  35.5 5.0 %all-to-all-start = ((bf16[16,64,1024]{2,1,0:T(8,128)(2,1)}), bf16[16,64,1024]{2,1,0:T(8,128)(2,1)}, u32[]{:S(2)}, u32[]{:S(2)}) async-start(bf16[16,64,1024]{2,1,0:T(8,128)(2,1)} %bitcast.87), calls=%async_computation | async-start | bytes 4194304 | tf_op jit(solution)/shard_map/all_to_all | solution.py:370
  40.6 2.8 collective-permute-start.1
  43.4 2.1 fusion.36
  45.5 77.6 %collective-permute-done.1 = bf16[256,1536]{1,0:T(8,128)(2,1)S(1)} collective-permute-done((bf16[256,1536]{1,0:T(8,128)(2,1)S(1)}, bf16[256,1536]{1,0:T(8,128)(2,1)S(1)}, u32[]{:S(2)}, u32[]{:S(2)}) %collective-permute-start.1) | collective-permute-done | bytes 786464 | tf_op jit(solution)/shard_map/ppermute | solution.py:308
  123.2 0.9 copy-done.15
  124.1 8.4 %mixer.1 = bf16[1024,1024]{1,0:T(8,128)(2,1)} custom-call(bf16[1024,1024]{1,0:T(8,128)(2,1)} %bitcast.17.refs_0_, bf16[4,512,256]{2,1,0:T(8,128)(2,1)} %select_convert_fusion.1.refs_1_, bf16[4,256,512]{2,1,0:T(8,128)(2,1)} %select_convert_fusion.refs_2_, bf16[8,256,256]{2,1,0:T(8,128)(2,1)} %get-tuple-element.30.refs_3_, ...), custom_call_target="tpu_custom_call" | custom-call | tf_op jit(solution)/shard_map/mixer/pallas_call | solution.py:187
  132.5 4.6 %all-to-all-start.1 = ((bf16[16,64,1024]{2,1,0:T(8,128)(2,1)}), bf16[16,64,1024]{2,1,0:T(8,128)(2,1)}, u32[]{:S(2)}, u32[]{:S(2)}) async-start(bf16[16,64,1024]{2,1,0:T(8,128)(2,1)} %bitcast.83), calls=%async_computation.1 | async-start | bytes 4194304 | tf_op jit(solution)/shard_map/all_to_all | solution.py:376
  137.3 2.8 collective-permute-start.2
  140.1 79.6 %collective-permute-done.2 = bf16[384,1024]{1,0:T(8,128)(2,1)S(1)} collective-permute-done((bf16[384,1024]{1,0:T(8,128)(2,1)}, bf16[384,1024]{1,0:T(8,128)(2,1)S(1)}, u32[]{:S(2)}, u32[]{:S(2)}) %collective-permute-start.2) | collective-permute-done | bytes 786464 | tf_op jit(solution)/shard_map/ppermute | solution.py:308
  219.7 0.9 copy-done.16
  220.6 5.0 %convert_reduce_fusion = (f32[1024]{0:T(1024)S(1)}, bf16[1024,1024]{1,0:T(8,128)(2,1)S(1)}) fusion(bf16[1024,1024]{1,0:T(8,128)(2,1)} %bitcast.21, bf16[128,8,8,128]{3,2,1,0:T(8,128)(2,1)} %bitcast.86, bf16[1,8,128,1024]{3,2,1,0:T(8,128)(2,1)S(1)} %copy-done.4), kind=kOutput, calls=%fused_computation.2 | convolution fusion | flops 2153774080 | bytes 8392704 | tf_op jit(solution)/shard_map/dot_general | solution.py:381
  227.1 1.3 fusion.33
  228.7 2.0 collective-permute-start.4
  230.7 1.0 copy.17.refs_1_
  231.8 0.8 slice_bitcast_fusion.6
  232.6 0.9 copy.18.refs_1_
  233.4 0.9 copy.19.refs_1_
  234.3 0.9 copy.20.refs_1_
  235.2 0.9 copy.21.refs_1_
  236.0 20.0 %ffn.6.refs_4_ = f32[1024,1024]{1,0:T(8,128)} custom-call(bf16[1024,1024]{1,0:T(8,128)(2,1)} %copy-done.2, f32[1024,1]{1,0:T(8,128)} %copy.17.refs_1_, bf16[2,1024,1536]{2,1,0:T(8,128)(2,1)} %bitcast.77, bf16[2,1536,1024]{2,1,0:T(8,128)(2,1)} %bitcast.80), custom_call_target="tpu_custom_call" | custom-call | tf_op jit(solution)/shard_map/ffn/pallas_call | solution.py:258
  256.0 1.0 copy-done.6
  257.0 11.9 %ffn.7.refs_4_ = f32[512,1024]{1,0:T(8,128)} custom-call(bf16[512,1024]{1,0:T(8,128)(2,1)} %copy-done.6, f32[512,1]{1,0:T(8,128)} %copy.18.refs_1_, bf16[2,1024,1536]{2,1,0:T(8,128)(2,1)} %bitcast.78, bf16[2,1536,1024]{2,1,0:T(8,128)(2,1)} %bitcast.81), custom_call_target="tpu_custom_call" | custom-call | tf_op jit(solution)/shard_map/ffn/pallas_call | solution.py:258
  268.9 7.1 %collective-permute-done.4.refs_0_ = bf16[512,1024]{1,0:T(8,128)(2,1)S(1)} collective-permute-done((bf16[512,1024]{1,0:T(8,128)(2,1)S(1)}, bf16[512,1024]{1,0:T(8,128)(2,1)S(1)}, u32[]{:S(2)}, u32[]{:S(2)}) %collective-permute-start.4) | collective-permute-done | bytes 1048608 | tf_op jit(solution)/shard_map/ppermute | solution.py:211
  276.0 1.0 copy-done.7
  277.0 11.9 %ffn.8.refs_4_ = f32[512,1024]{1,0:T(8,128)} custom-call(bf16[512,1024]{1,0:T(8,128)(2,1)} %copy-done.7, f32[512,1]{1,0:T(8,128)} %copy.19.refs_1_, bf16[2,1024,1536]{2,1,0:T(8,128)(2,1)} %bitcast.79, bf16[2,1536,1024]{2,1,0:T(8,128)(2,1)} %bitcast.82), custom_call_target="tpu_custom_call" | custom-call | tf_op jit(solution)/shard_map/ffn/pallas_call | solution.py:258
  288.8 12.6 %ffn.9 = bf16[512,1024]{1,0:T(8,128)(2,1)} custom-call(bf16[512,1024]{1,0:T(8,128)(2,1)} %copy-done.6, f32[512,1]{1,0:T(8,128)} %copy.20.refs_1_, bf16[2,1024,1536]{2,1,0:T(8,128)(2,1)} %bitcast.71, bf16[2,1536,1024]{2,1,0:T(8,128)(2,1)} %bitcast.74, f32[512,1024]{1,0:T(8,128)} %ffn.7.refs_4_), custom_call_target="tpu_custom_call" | custom-call | tf_op jit(solution)/shard_map/ffn/pallas_call | solution.py:258
  301.4 12.5 %ffn.10 = bf16[512,1024]{1,0:T(8,128)(2,1)} custom-call(bf16[512,1024]{1,0:T(8,128)(2,1)} %copy-done.7, f32[512,1]{1,0:T(8,128)} %copy.21.refs_1_, bf16[2,1024,1536]{2,1,0:T(8,128)(2,1)} %bitcast.72, bf16[2,1536,1024]{2,1,0:T(8,128)(2,1)} %bitcast.75, f32[512,1024]{1,0:T(8,128)} %ffn.8.refs_4_), custom_call_target="tpu_custom_call" | custom-call | tf_op jit(solution)/shard_map/ffn/pallas_call | solution.py:258
  314.1 1.7 collective-permute-start.5
  315.9 1.1 copy.22.refs_1_
  317.0 20.3 %ffn.11 = f32[1024,1024]{1,0:T(8,128)} custom-call(bf16[1024,1024]{1,0:T(8,128)(2,1)} %copy-done.2, f32[1024,1]{1,0:T(8,128)} %copy.22.refs_1_, bf16[2,1024,1536]{2,1,0:T(8,128)(2,1)} %bitcast.73, bf16[2,1536,1024]{2,1,0:T(8,128)(2,1)} %bitcast.76, f32[1024,1024]{1,0:T(8,128)} %ffn.6.refs_4_), custom_call_target="tpu_custom_call" | custom-call | tf_op jit(solution)/shard_map/ffn/pallas_call | solution.py:258
  337.3 2.9 collective-permute-done.6
  340.2 20.2 %collective-permute-done.5 = bf16[512,1024]{1,0:T(8,128)(2,1)} collective-permute-done((bf16[512,1024]{1,0:T(8,128)(2,1)S(1)}, bf16[512,1024]{1,0:T(8,128)(2,1)}, u32[]{:S(2)}, u32[]{:S(2)}) %collective-permute-start.5) | collective-permute-done | bytes 1048608 | tf_op jit(solution)/shard_map/ppermute | solution.py:211
  360.4 6.0 %fusion.6 = bf16[1024,1024]{1,0:T(8,128)(2,1)} fusion(f32[1024,1024]{1,0:T(8,128)} %ffn.11, bf16[1024,1024]{1,0:T(8,128)(2,1)} %copy-done.5, bf16[512,1024]{1,0:T(8,128)(2,1)} %collective-permute-done.6, bf16[512,1024]{1,0:T(8,128)(2,1)} %collective-permute-done.5), kind=kLoop, calls=%fused_computation.9 | loop fusion | flops 8388608 | bytes 10485760 | tf_op jit(solution)/shard_map/convert_element_type | solution.py:420
  (86 shorter events, 9.1 us)
Async XLA Ops:
  6.5 1.9 copy-start
  6.5 229.5 %all-gather.11.cloned.1.call-start = ((), (), s32[]{:S(2)}) async-start(), calls=%async_computation.4 | async-start | bytes 7077888 | tf_op jit(solution)/shard_map/all_gather | solution.py:304
  8.4 3.2 copy-start.19
  8.4 3.2 copy-start.20
  9.4 226.6 %all-gather.13.cloned.1.call-start = ((), (), s32[]{:S(2)}) async-start(), calls=%async_computation.5 | async-start | bytes 7077888 | tf_op jit(solution)/shard_map/all_gather | solution.py:304
  12.9 22.6 %collective-permute-start = (f32[2,1024]{1,0:T(2,128)}, f32[2,1024]{1,0:T(2,128)}, u32[]{:S(2)}, u32[]{:S(2)}) collective-permute-start(f32[2,1024]{1,0:T(2,128)} %pad_maximum_fusion), channel_id=1, source_target_pairs={{0,4},{4,0},{1,5},{5,1},{2,6},{6,2},{3,7},{7,3},{8,12},{12,8},{9,1... | collective-permute-start | bytes 24584 | tf_op jit(solution)/shard_map/ppermute | solution.py:211
  20.0 3.2 copy-start.9
  23.2 2.4 copy-start.3
  25.5 1.1 copy-start.21
  25.5 1.2 copy-start.13
  25.5 1.2 copy-start.14
  25.9 2.0 copy-start.11
  25.9 2.0 copy-start.12
  27.9 1.9 copy-start.22
  29.8 1.4 copy-start.8
  35.5 87.7 %all-to-all-start = ((bf16[16,64,1024]{2,1,0:T(8,128)(2,1)}), bf16[16,64,1024]{2,1,0:T(8,128)(2,1)}, u32[]{:S(2)}, u32[]{:S(2)}) async-start(bf16[16,64,1024]{2,1,0:T(8,128)(2,1)} %bitcast.87), calls=%async_computation | async-start | bytes 4194304 | tf_op jit(solution)/shard_map/all_to_all | solution.py:370
  40.5 248.4 %all-gather.7.cloned.1.call-start = ((), (), s32[]{:S(2)}) async-start(), calls=%async_computation.2 | async-start | bytes 7077888 | tf_op jit(solution)/shard_map/all_gather | solution.py:304
  40.6 82.6 %collective-permute-start.1 = (bf16[256,1536]{1,0:T(8,128)(2,1)S(1)}, bf16[256,1536]{1,0:T(8,128)(2,1)S(1)}, u32[]{:S(2)}, u32[]{:S(2)}) collective-permute-start(bf16[256,1536]{1,0:T(8,128)(2,1)S(1)} %fusion.37), channel_id=1, source_target_pairs={{0,8},{8,0},{1,9},{9,1},{2,10},{10,2},{3,11},{11,3},{4,12},{12,4},... | collective-permute-start | bytes 2359304 | tf_op jit(solution)/shard_map/ppermute | solution.py:308
  123.2 0.9 copy-start.15
  132.5 88.1 %copy-start.4 = (bf16[1,8,128,1024]{3,2,1,0:T(8,128)(2,1)S(1)}, bf16[1,8,128,1024]{3,2,1,0:T(8,128)(2,1)}, u32[]{:S(2)}) copy-start(bf16[1,8,128,1024]{3,2,1,0:T(8,128)(2,1)} %param.10) | copy-start | bytes 6291460
  132.5 87.2 %all-to-all-start.1 = ((bf16[16,64,1024]{2,1,0:T(8,128)(2,1)}), bf16[16,64,1024]{2,1,0:T(8,128)(2,1)}, u32[]{:S(2)}, u32[]{:S(2)}) async-start(bf16[16,64,1024]{2,1,0:T(8,128)(2,1)} %bitcast.83), calls=%async_computation.1 | async-start | bytes 4194304 | tf_op jit(solution)/shard_map/all_to_all | solution.py:376
  137.1 151.7 %all-gather.9.cloned.1.call-start = ((), (), s32[]{:S(2)}) async-start(), calls=%async_computation.3 | async-start | bytes 7077888 | tf_op jit(solution)/shard_map/all_gather | solution.py:304
  137.3 82.4 %collective-permute-start.2 = (bf16[384,1024]{1,0:T(8,128)(2,1)}, bf16[384,1024]{1,0:T(8,128)(2,1)S(1)}, u32[]{:S(2)}, u32[]{:S(2)}) collective-permute-start(bf16[384,1024]{1,0:T(8,128)(2,1)} %fusion.36), channel_id=1, source_target_pairs={{0,8},{8,0},{1,9},{9,1},{2,10},{10,2},{3,11},{11,3},{4,12},{12,4},... | collective-permute-start | bytes 2359304 | tf_op jit(solution)/shard_map/ppermute | solution.py:308
  219.7 0.9 copy-start.16
  225.6 1.4 copy-start.5
  225.6 0.7 copy-start.23
  227.1 1.7 copy-start.2
  227.1 3.7 copy-start.18
  228.7 27.3 %collective-permute-start.3 = (bf16[512,1024]{1,0:T(8,128)(2,1)}, bf16[512,1024]{1,0:T(8,128)(2,1)S(1)}, u32[]{:S(2)}, u32[]{:S(2)}) collective-permute-start(bf16[512,1024]{1,0:T(8,128)(2,1)} %get-tuple-element.52), channel_id=1, source_target_pairs={{0,4},{4,0},{1,5},{5,1},{2,6},{6,2},{3,7},{7,3},{8,12},{12,8},{9,1... | collective-permute-start | bytes 3145736 | tf_op jit(solution)/shard_map/ppermute | solution.py:211
  228.7 47.3 %collective-permute-start.4 = (bf16[512,1024]{1,0:T(8,128)(2,1)S(1)}, bf16[512,1024]{1,0:T(8,128)(2,1)S(1)}, u32[]{:S(2)}, u32[]{:S(2)}) collective-permute-start(bf16[512,1024]{1,0:T(8,128)(2,1)S(1)} %get-tuple-element.51), channel_id=1, source_target_pairs={{0,4},{4,0},{1,5},{5,1},{2,6},{6,2},{3,7},{7,3},{8,12},{12,8},{9,1... | collective-permute-start | bytes 3145736 | tf_op jit(solution)/shard_map/ppermute | solution.py:211
  256.0 1.0 copy-start.6
  276.0 1.0 copy-start.7
  301.4 12.7 %copy-start.10 = (bf16[512,1024]{1,0:T(8,128)(2,1)S(1)}, bf16[512,1024]{1,0:T(8,128)(2,1)}, u32[]{:S(2)}) copy-start(bf16[512,1024]{1,0:T(8,128)(2,1)} %ffn.9) | copy-start | bytes 3145732
  301.4 14.5 %copy-start.17 = (f32[8,128]{1,0:T(8,128)S(1)}, f32[8,128]{1,0:T(8,128)}, u32[]{:S(2)}) copy-start(f32[8,128]{1,0:T(8,128)} %get-tuple-element.47) | copy-start | bytes 12292
  313.9 26.3 %collective-permute-start.6 = (bf16[512,1024]{1,0:T(8,128)(2,1)}, bf16[512,1024]{1,0:T(8,128)(2,1)}, u32[]{:S(2)}, u32[]{:S(2)}) collective-permute-start(bf16[512,1024]{1,0:T(8,128)(2,1)} %ffn.10), channel_id=1, source_target_pairs={{0,4},{4,0},{1,5},{5,1},{2,6},{6,2},{3,7},{7,3},{8,12},{12,8},{9,1... | collective-permute-start | bytes 3145736 | tf_op jit(solution)/shard_map/ppermute | solution.py:211
  314.1 46.3 %collective-permute-start.5 = (bf16[512,1024]{1,0:T(8,128)(2,1)S(1)}, bf16[512,1024]{1,0:T(8,128)(2,1)}, u32[]{:S(2)}, u32[]{:S(2)}) collective-permute-start(bf16[512,1024]{1,0:T(8,128)(2,1)S(1)} %copy-done.10), channel_id=1, source_target_pairs={{0,4},{4,0},{1,5},{5,1},{2,6},{6,2},{3,7},{7,3},{8,12},{12,8},{9,1... | collective-permute-start | bytes 3145736 | tf_op jit(solution)/shard_map/ppermute | solution.py:211
  360.4 6.0 %copy-start.1 = (bf16[1,1024,1536]{2,1,0:T(8,128)(2,1)S(1)}, bf16[1,1024,1536]{2,1,0:T(8,128)(2,1)}, u32[]{:S(2)}) copy-start(bf16[1,1024,1536]{2,1,0:T(8,128)(2,1)} %param.18) | copy-start | bytes 9437188
Sparse Core Ops, SparseCore 0:
  9.5 64.9 all-gather.10
  76.4 50.9 all-gather.12
  129.4 65.8 all-gather.6
  220.7 44.3 all-gather.8
